TPU v7x, 512 devices: a whole 4x8x8 slice. The times are simulated.
512 devices in a mesh: face: 128 (over y_hi, z, x), chan: 4 (over y_lo, core).
Axes of the slice: x: 4, y: 8 (y_hi: 4, y_lo: 2; y = y_hi * 2 + y_lo), z: 8, core: 2. Of those that a mesh axis runs over, the one named last changes fastest.
Arguments:
- field_in: bfloat16 [256, 131072], P('chan', 'face'), may hold values from -6 to 6
- edge_codes: int32 [128, 4], replicated, may hold values from 0 to 7
- weight_enc: bfloat16 [9, 256, 256], P(None, 'chan'), may hold values from -0.125 to 0.125
- bias_enc: float32 [256], P('chan'), may hold values from -3 to 3
- weight_mid_a: bfloat16 [9, 256, 256], P(None, 'chan'), may hold values from -0.125 to 0.125
- bias_mid_a: float32 [256], P('chan'), may hold values from -3 to 3
- weight_mid_b: bfloat16 [9, 256, 256], P(None, 'chan'), may hold values from -0.125 to 0.125
- bias_mid_b: float32 [256], P('chan'), may hold values from -3 to 3
- weight_dec: bfloat16 [9, 256, 256], P(None, 'chan'), may hold values from -0.125 to 0.125
- bias_dec: float32 [256], P('chan'), may hold values from -3 to 3
Outputs:
- field_out: bfloat16 [256, 131072], P('chan', 'face')
Inputs may be any that keep to these rules, and one draw needn't show every extreme that they name: edge_codes[t, s] mod 4 names the edge (0 top row, 1 bottom row, 2 left column, 3 right column) of tile t's neighbour on side s that borders it; a value of 4 or more means that edge is read in reverse order.
All inputs are finite; a program needn't handle non-finite values.
Results may differ from a plain program's by a relative error of at most 0.012.
Values may be sent and summed in bfloat16 or wider, within the bound.
A program may use at most 64 MiB of HBM per device.

v0:
```python
import jax
import jax.numpy as jnp
from jax import lax
from jax.sharding import PartitionSpec as P

B = 32
TILE_COLS = 4


def shifted(array, axis, by):
    peers = lax.axis_size(axis)
    return lax.ppermute(array, axis, [(i, (i + by) % peers) for i in range(peers)])


def orient(edge_code, source):
    picked = lax.dynamic_index_in_dim(source, edge_code % 4, 0, keepdims=False)
    return jnp.where(edge_code >= 4, picked[:, ::-1], picked)


def face_rims(border_rows, edge_codes):
    position = lax.axis_index("face")
    north_rim = orient(edge_codes[position, 0], shifted(border_rows, "face", TILE_COLS))
    south_rim = orient(edge_codes[position, 1], shifted(border_rows, "face", -TILE_COLS))
    west_rim = orient(edge_codes[position, 2], shifted(border_rows, "face", 1))
    east_rim = orient(edge_codes[position, 3], shifted(border_rows, "face", -1))
    return (north_rim, south_rim, west_rim, east_rim)


def with_rims(fields, edge_codes):
    extent = fields.shape[-1]
    border_rows = jnp.stack(
        [fields[:, 0, :], fields[:, extent - 1, :], fields[:, :, 0], fields[:, :, extent - 1]],
        axis=0,
    )
    north_rim, south_rim, west_rim, east_rim = face_rims(border_rows, edge_codes)
    middle = jnp.concatenate([west_rim[:, :, None], fields, east_rim[:, :, None]], axis=2)
    top_row = jnp.pad(north_rim, ((0, 0), (1, 1)))[:, None, :]
    bottom = jnp.pad(south_rim, ((0, 0), (1, 1)))[:, None, :]
    padded = jnp.concatenate([top_row, middle, bottom], axis=1)
    return jnp.pad(padded.reshape(fields.shape[0], -1), ((0, 0), (0, 2)))


def convolve_flat(flattened, weights, row_count, width):
    padded_width = width + 2
    out_length = row_count * padded_width
    running = jnp.zeros((weights.shape[1], out_length), jnp.float32)
    for kernel_tap in range(9):
        offset = kernel_tap // 3 * padded_width + kernel_tap % 3
        running = running + jnp.dot(
            weights[kernel_tap],
            flattened[:, offset : offset + out_length],
            preferred_element_type=jnp.float32,
        )
    return running


def finish_block(fields, running, bias_vec, row_count, width):
    convolved = running.reshape(-1, row_count, width + 2)[:, :, :width] + bias_vec[:, None, None]
    return (fields.astype(jnp.float32) + jax.nn.gelu(convolved, approximate=True)).astype(
        jnp.bfloat16
    )


def conv_block(fields, edge_codes, weights, bias_vec):
    extent = fields.shape[-1]
    gathered = lax.all_gather(fields, "chan", axis=0, tiled=True)
    running = convolve_flat(with_rims(gathered, edge_codes), weights, extent, extent)
    return finish_block(fields, running, bias_vec, extent, extent)


def unet_window(fields, edge_codes, kernels, block_fn):
    (
        weight_enc,
        weight_mid_a,
        weight_mid_b,
        weight_dec,
        bias_enc,
        bias_mid_a,
        bias_mid_b,
        bias_dec,
    ) = kernels
    channels, row_count, width = fields.shape
    encoded = block_fn(fields, edge_codes, weight_enc, bias_enc)
    coarse = (
        encoded.astype(jnp.float32)
        .reshape(channels, row_count // 2, 2, width // 2, 2)
        .mean(axis=(2, 4))
        .astype(jnp.bfloat16)
    )
    middle_a = block_fn(coarse, edge_codes, weight_mid_a, bias_mid_a)
    middle_b = block_fn(middle_a, edge_codes, weight_mid_b, bias_mid_b)
    refined = jnp.repeat(jnp.repeat(middle_b, 2, axis=1), 2, axis=2)
    joined = (refined.astype(jnp.float32) + encoded.astype(jnp.float32)).astype(jnp.bfloat16)
    return block_fn(joined, edge_codes, weight_dec, bias_dec)


def on_device(
    field_in,
    edge_codes,
    weight_enc,
    bias_enc,
    weight_mid_a,
    bias_mid_a,
    weight_mid_b,
    bias_mid_b,
    weight_dec,
    bias_dec,
):
    channels = field_in.shape[0]
    kernels = (
        weight_enc,
        weight_mid_a,
        weight_mid_b,
        weight_dec,
        bias_enc,
        bias_mid_a,
        bias_mid_b,
        bias_dec,
    )
    fields = field_in.reshape(channels, B, B)
    result = unet_window(fields, edge_codes, kernels, conv_block)
    return result.reshape(channels, B * B)


def solution(mesh):
    in_specs = (
        P("chan", "face"),
        P(),
        P(None, "chan", None),
        P("chan"),
        P(None, "chan", None),
        P("chan"),
        P(None, "chan", None),
        P("chan"),
        P(None, "chan", None),
        P("chan"),
    )
    out_specs = P("chan", "face")
    return jax.shard_map(
        on_device, mesh=mesh, in_specs=in_specs, out_specs=out_specs, check_vma=False
    )
```

profile of v0, /device:TPU:1, one launch (start us, length us, event | category | flops | bytes accessed | tf_op | source)
XLA Modules:
  0.0 250.5 jit_solution(146410013715689471)
XLA Ops:
  0.0 1.1 copy.153
  1.1 0.8 copy.154
  1.9 19.0 %all_gather.12 = bf16[256,32,32]{2,1,0:T(8,128)(2,1)S(1)} all-gather(bf16[64,32,32]{2,1,0:T(8,128)(2,1)S(1)} %copy.154), channel_id=1, replica_groups=mesh['face'=128,'chan'=4] {'chan'}, dimensions={0}, use_global_device_ids=true | all-gather | bytes 655360 | tf_op jit(solution)/shard_map/all_gather | solution.py:66
  21.1 2.9 %fusion.166 = (bf16[256,32,1]{2,1,0:T(8,128)(2,1)}, bf16[256,32,1]{2,1,0:T(8,128)(2,1)}) fusion(bf16[256,32,32]{2,1,0:T(8,128)(2,1)S(1)} %all_gather.12), kind=kLoop, calls=%fused_computation.268 | loop fusion | bytes 65536 | tf_op jit(solution)/shard_map/slice | solution.py:32
  24.1 3.3 %copy.195 = bf16[256,32,1]{0,1,2:T(8,128)(2,1)S(1)} copy(bf16[256,32,1]{2,1,0:T(8,128)(2,1)} %get-tuple-element.11) | data formatting | bytes 32768
  27.4 3.3 %copy.196 = bf16[256,32,1]{0,1,2:T(8,128)(2,1)S(1)} copy(bf16[256,32,1]{2,1,0:T(8,128)(2,1)} %get-tuple-element.12) | data formatting | bytes 32768
  30.7 12.0 %collective-permute-start.3 = (bf16[4,256,32]{1,2,0:T(8,128)(2,1)S(1)}, bf16[4,256,32]{1,2,0:T(8,128)(2,1)S(1)}, u32[]{:S(2)}, u32[]{:S(2)}) collective-permute-start(bf16[4,256,32]{1,2,0:T(8,128)(2,1)S(1)} %pad_maximum_fusion.8), channel_id=1, source_target_pairs={{0,496},{4,500},{8,504},{12,508},{16,0},{20,4},{24,8},{28,12},{32,... | collective-permute-start | bytes 196616 | tf_op jit(solution)/shard_map/ppermute | solution.py:12
  42.7 4.4 %collective-permute-start.2 = (bf16[4,256,32]{1,2,0:T(8,128)(2,1)S(1)}, bf16[4,256,32]{1,2,0:T(8,128)(2,1)S(1)}, u32[]{:S(2)}, u32[]{:S(2)}) collective-permute-start(bf16[4,256,32]{1,2,0:T(8,128)(2,1)S(1)} %pad_maximum_fusion.8), channel_id=1, source_target_pairs={{0,508},{4,0},{8,4},{12,8},{16,12},{20,16},{24,20},{28,24},{32,28}... | collective-permute-start | bytes 196616 | tf_op jit(solution)/shard_map/ppermute | solution.py:12
  47.1 1.9 collective-permute-start.1
  49.0 3.4 %collective-permute-start = (bf16[4,256,32]{1,2,0:T(8,128)(2,1)S(1)}, bf16[4,256,32]{1,2,0:T(8,128)(2,1)S(1)}, u32[]{:S(2)}, u32[]{:S(2)}) collective-permute-start(bf16[4,256,32]{1,2,0:T(8,128)(2,1)S(1)} %pad_maximum_fusion.8), channel_id=1, source_target_pairs={{0,16},{4,20},{8,24},{12,28},{16,32},{20,36},{24,40},{28,44},{32,4... | collective-permute-start | bytes 196616 | tf_op jit(solution)/shard_map/ppermute | solution.py:12
  52.4 0.7 constant_dynamic-slice_fusion
  63.5 3.9 %copy.159 = bf16[256,32,1]{2,1,0:T(8,128)(2,1)} copy(bf16[256,32,1]{0,1,2:T(8,128)(2,1)S(1)} %select_bitcast_fusion.3) | data formatting | bytes 32768 | tf_op jit(solution)/shard_map/broadcast_in_dim | solution.py:36
  67.4 3.9 %copy.160 = bf16[256,32,1]{2,1,0:T(8,128)(2,1)} copy(bf16[256,32,1]{0,1,2:T(8,128)(2,1)S(1)} %select_bitcast_fusion.2) | data formatting | bytes 32768 | tf_op jit(solution)/shard_map/broadcast_in_dim | solution.py:36
  71.3 5.5 %pad_maximum_fusion = bf16[256,32,34]{2,1,0:T(8,128)(2,1)} fusion(bf16[256,32,1]{2,1,0:T(8,128)(2,1)} %copy.160, bf16[256,32,32]{2,1,0:T(8,128)(2,1)S(1)} %all_gather.12, bf16[256,32,1]{2,1,0:T(8,128)(2,1)} %copy.159), kind=kLoop, calls=%fused_computation.18 | loop fusion | flops 1671168 | bytes 1114112 | tf_op jit(solution)/shard_map/concatenate | solution.py:36
  76.8 3.3 %copy.161 = bf16[256,32,34]{0,2,1:T(8,128)(2,1)S(1)} copy(bf16[256,32,34]{2,1,0:T(8,128)(2,1)} %pad_maximum_fusion) | data formatting | bytes 1114112 | tf_op jit(solution)/shard_map/concatenate | solution.py:36
  80.4 0.6 copy-done
  81.3 0.3 convolution_add_fusion.15
  84.3 0.4 reduce_sum.9
  85.0 10.8 %all_gather.13 = bf16[256,16,16]{2,1,0:T(8,128)(2,1)S(1)} all-gather(bf16[64,16,16]{2,1,0:T(8,128)(2,1)S(1)} %copy.163), channel_id=1, replica_groups=mesh['face'=128,'chan'=4] {'chan'}, dimensions={0}, use_global_device_ids=true | all-gather | bytes 163840 | tf_op jit(solution)/shard_map/all_gather | solution.py:66
  96.0 1.5 fusion.170
  97.7 2.2 copy.199
  99.9 0.9 copy.200
  100.8 6.4 %collective-permute-start.7 = (bf16[4,256,16]{1,2,0:T(8,128)(2,1)S(1)}, bf16[4,256,16]{1,2,0:T(8,128)(2,1)S(1)}, u32[]{:S(2)}, u32[]{:S(2)}) collective-permute-start(bf16[4,256,16]{1,2,0:T(8,128)(2,1)S(1)} %pad_maximum_fusion.10), channel_id=1, source_target_pairs={{0,496},{4,500},{8,504},{12,508},{16,0},{20,4},{24,8},{28,12},{32,... | collective-permute-start | bytes 98312 | tf_op jit(solution)/shard_map/ppermute | solution.py:12
  107.2 5.7 %collective-permute-start.6 = (bf16[4,256,16]{1,2,0:T(8,128)(2,1)S(1)}, bf16[4,256,16]{1,2,0:T(8,128)(2,1)S(1)}, u32[]{:S(2)}, u32[]{:S(2)}) collective-permute-start(bf16[4,256,16]{1,2,0:T(8,128)(2,1)S(1)} %pad_maximum_fusion.10), channel_id=1, source_target_pairs={{0,508},{4,0},{8,4},{12,8},{16,12},{20,16},{24,20},{28,24},{32,28}... | collective-permute-start | bytes 98312 | tf_op jit(solution)/shard_map/ppermute | solution.py:12
  113.0 1.9 collective-permute-start.5
  114.9 3.1 %collective-permute-start.4 = (bf16[4,256,16]{1,2,0:T(8,128)(2,1)S(1)}, bf16[4,256,16]{1,2,0:T(8,128)(2,1)S(1)}, u32[]{:S(2)}, u32[]{:S(2)}) collective-permute-start(bf16[4,256,16]{1,2,0:T(8,128)(2,1)S(1)} %pad_maximum_fusion.10), channel_id=1, source_target_pairs={{0,16},{4,20},{8,24},{12,28},{16,32},{20,36},{24,40},{28,44},{32,4... | collective-permute-start | bytes 98312 | tf_op jit(solution)/shard_map/ppermute | solution.py:12
  118.2 6.1 %collective-permute-done.5 = bf16[4,256,16]{1,2,0:T(8,128)(2,1)S(1)} collective-permute-done((bf16[4,256,16]{1,2,0:T(8,128)(2,1)S(1)}, bf16[4,256,16]{1,2,0:T(8,128)(2,1)S(1)}, u32[]{:S(2)}, u32[]{:S(2)}) %collective-permute-start.5) | collective-permute-done | bytes 32800 | tf_op jit(solution)/shard_map/ppermute | solution.py:12
  124.6 1.0 copy.168
  125.6 1.9 copy.169
  127.5 3.2 %pad_maximum_fusion.2 = bf16[256,16,18]{2,1,0:T(8,128)(2,1)} fusion(bf16[256,16,1]{2,1,0:T(8,128)(2,1)} %copy.169, bf16[256,16,16]{2,1,0:T(8,128)(2,1)S(1)} %all_gather.13, bf16[256,16,1]{2,1,0:T(8,128)(2,1)S(1)} %copy.168), kind=kLoop, calls=%fused_computation.38 | loop fusion | flops 442368 | bytes 294912 | tf_op jit(solution)/shard_map/concatenate | solution.py:36
  130.7 2.2 copy.170
  135.4 11.0 %all_gather.14 = bf16[256,16,16]{2,1,0:T(8,128)(2,1)S(1)} all-gather(bf16[64,16,16]{2,1,0:T(8,128)(2,1)S(1)} %copy.172), channel_id=1, replica_groups=mesh['face'=128,'chan'=4] {'chan'}, dimensions={0}, use_global_device_ids=true | all-gather | bytes 163840 | tf_op jit(solution)/shard_map/all_gather | solution.py:66
  146.7 1.5 fusion.168
  148.3 2.2 copy.203
  150.5 0.9 copy.204
  151.4 1.9 collective-permute-start.11
  153.4 5.4 %collective-permute-start.10 = (bf16[4,256,16]{1,2,0:T(8,128)(2,1)S(1)}, bf16[4,256,16]{1,2,0:T(8,128)(2,1)S(1)}, u32[]{:S(2)}, u32[]{:S(2)}) collective-permute-start(bf16[4,256,16]{1,2,0:T(8,128)(2,1)S(1)} %pad_maximum_fusion.11), channel_id=1, source_target_pairs={{0,508},{4,0},{8,4},{12,8},{16,12},{20,16},{24,20},{28,24},{32,28}... | collective-permute-start | bytes 98312 | tf_op jit(solution)/shard_map/ppermute | solution.py:12
  158.8 1.9 collective-permute-start.9
  160.7 3.5 %collective-permute-start.8 = (bf16[4,256,16]{1,2,0:T(8,128)(2,1)S(1)}, bf16[4,256,16]{1,2,0:T(8,128)(2,1)S(1)}, u32[]{:S(2)}, u32[]{:S(2)}) collective-permute-start(bf16[4,256,16]{1,2,0:T(8,128)(2,1)S(1)} %pad_maximum_fusion.11), channel_id=1, source_target_pairs={{0,16},{4,20},{8,24},{12,28},{16,32},{20,36},{24,40},{28,44},{32,4... | collective-permute-start | bytes 98312 | tf_op jit(solution)/shard_map/ppermute | solution.py:12
  164.4 5.3 %collective-permute-done.9 = bf16[4,256,16]{1,2,0:T(8,128)(2,1)S(1)} collective-permute-done((bf16[4,256,16]{1,2,0:T(8,128)(2,1)S(1)}, bf16[4,256,16]{1,2,0:T(8,128)(2,1)S(1)}, u32[]{:S(2)}, u32[]{:S(2)}) %collective-permute-start.9) | collective-permute-done | bytes 32800 | tf_op jit(solution)/shard_map/ppermute | solution.py:12
  170.0 1.0 copy.177
  171.1 1.9 copy.178
  173.0 3.2 %pad_maximum_fusion.3 = bf16[256,16,18]{2,1,0:T(8,128)(2,1)} fusion(bf16[256,16,1]{2,1,0:T(8,128)(2,1)} %copy.178, bf16[256,16,16]{2,1,0:T(8,128)(2,1)S(1)} %all_gather.14, bf16[256,16,1]{2,1,0:T(8,128)(2,1)S(1)} %copy.177), kind=kLoop, calls=%fused_computation.39 | loop fusion | flops 442368 | bytes 294912 | tf_op jit(solution)/shard_map/concatenate | solution.py:36
  176.2 2.2 copy.179
  180.9 0.3 fusion.42
  181.2 0.8 copy.183
  182.0 16.6 %all_gather.15 = bf16[256,32,32]{2,1,0:T(8,128)(2,1)S(1)} all-gather(bf16[64,32,32]{2,1,0:T(8,128)(2,1)S(1)} %copy.183), channel_id=1, replica_groups=mesh['face'=128,'chan'=4] {'chan'}, dimensions={0}, use_global_device_ids=true | all-gather | bytes 655360 | tf_op jit(solution)/shard_map/all_gather | solution.py:66
  198.8 2.9 %fusion.164 = (bf16[256,32,1]{2,1,0:T(8,128)(2,1)}, bf16[256,32,1]{2,1,0:T(8,128)(2,1)}) fusion(bf16[256,32,32]{2,1,0:T(8,128)(2,1)S(1)} %all_gather.15), kind=kLoop, calls=%fused_computation.266 | loop fusion | bytes 65536 | tf_op jit(solution)/shard_map/slice | solution.py:32
  201.9 3.3 %copy.207 = bf16[256,32,1]{0,1,2:T(8,128)(2,1)S(1)} copy(bf16[256,32,1]{2,1,0:T(8,128)(2,1)} %get-tuple-element.7) | data formatting | bytes 32768
  205.1 3.3 %copy.208 = bf16[256,32,1]{0,1,2:T(8,128)(2,1)S(1)} copy(bf16[256,32,1]{2,1,0:T(8,128)(2,1)} %get-tuple-element.8) | data formatting | bytes 32768
  208.4 1.9 collective-permute-start.15
  210.3 5.4 %collective-permute-start.14 = (bf16[4,256,32]{1,2,0:T(8,128)(2,1)S(1)}, bf16[4,256,32]{1,2,0:T(8,128)(2,1)S(1)}, u32[]{:S(2)}, u32[]{:S(2)}) collective-permute-start(bf16[4,256,32]{1,2,0:T(8,128)(2,1)S(1)} %pad_maximum_fusion.9), channel_id=1, source_target_pairs={{0,508},{4,0},{8,4},{12,8},{16,12},{20,16},{24,20},{28,24},{32,28}... | collective-permute-start | bytes 196616 | tf_op jit(solution)/shard_map/ppermute | solution.py:12
  215.7 1.9 collective-permute-start.13
  217.7 3.9 %collective-permute-start.12 = (bf16[4,256,32]{1,2,0:T(8,128)(2,1)S(1)}, bf16[4,256,32]{1,2,0:T(8,128)(2,1)S(1)}, u32[]{:S(2)}, u32[]{:S(2)}) collective-permute-start(bf16[4,256,32]{1,2,0:T(8,128)(2,1)S(1)} %pad_maximum_fusion.9), channel_id=1, source_target_pairs={{0,16},{4,20},{8,24},{12,28},{16,32},{20,36},{24,40},{28,44},{32,4... | collective-permute-start | bytes 196616 | tf_op jit(solution)/shard_map/ppermute | solution.py:12
  221.8 7.3 %collective-permute-done.13 = bf16[4,256,32]{1,2,0:T(8,128)(2,1)S(1)} collective-permute-done((bf16[4,256,32]{1,2,0:T(8,128)(2,1)S(1)}, bf16[4,256,32]{1,2,0:T(8,128)(2,1)S(1)}, u32[]{:S(2)}, u32[]{:S(2)}) %collective-permute-start.13) | collective-permute-done | bytes 65568 | tf_op jit(solution)/shard_map/ppermute | solution.py:12
  229.3 3.9 %copy.188 = bf16[256,32,1]{2,1,0:T(8,128)(2,1)} copy(bf16[256,32,1]{0,1,2:T(8,128)(2,1)S(1)} %select_bitcast_fusion.1) | data formatting | bytes 32768 | tf_op jit(solution)/shard_map/broadcast_in_dim | solution.py:36
  233.2 3.9 %copy.189 = bf16[256,32,1]{2,1,0:T(8,128)(2,1)} copy(bf16[256,32,1]{0,1,2:T(8,128)(2,1)S(1)} %select_bitcast_fusion) | data formatting | bytes 32768 | tf_op jit(solution)/shard_map/broadcast_in_dim | solution.py:36
  237.1 5.5 %pad_maximum_fusion.1 = bf16[256,32,34]{2,1,0:T(8,128)(2,1)} fusion(bf16[256,32,1]{2,1,0:T(8,128)(2,1)} %copy.189, bf16[256,32,32]{2,1,0:T(8,128)(2,1)S(1)} %all_gather.15, bf16[256,32,1]{2,1,0:T(8,128)(2,1)} %copy.188), kind=kLoop, calls=%fused_computation.19 | loop fusion | flops 1671168 | bytes 1114112 | tf_op jit(solution)/shard_map/concatenate | solution.py:36
  242.6 3.4 %copy.190 = bf16[256,32,34]{0,2,1:T(8,128)(2,1)S(1)} copy(bf16[256,32,34]{2,1,0:T(8,128)(2,1)} %pad_maximum_fusion.1) | data formatting | bytes 1114112 | tf_op jit(solution)/shard_map/concatenate | solution.py:36
  246.5 0.3 convolution_add_fusion.7
  246.8 0.3 convolution_add_fusion.6
  247.5 0.3 convolution_add_fusion.4
  247.8 0.3 convolution_add_fusion.3
  249.5 0.8 copy.192
  (158 shorter events, 13.3 us)
Async XLA Ops:
  24.1 28.3 %copy-start.4 = (s32[128,4]{0,1:T(4,128)S(1)}, s32[128,4]{0,1:T(4,128)}, u32[]{:S(2)}) copy-start(s32[128,4]{0,1:T(4,128)} %param.11) | copy-start | bytes 6148
  30.7 32.3 %collective-permute-start.3 = (bf16[4,256,32]{1,2,0:T(8,128)(2,1)S(1)}, bf16[4,256,32]{1,2,0:T(8,128)(2,1)S(1)}, u32[]{:S(2)}, u32[]{:S(2)}) collective-permute-start(bf16[4,256,32]{1,2,0:T(8,128)(2,1)S(1)} %pad_maximum_fusion.8), channel_id=1, source_target_pairs={{0,496},{4,500},{8,504},{12,508},{16,0},{20,4},{24,8},{28,12},{32,... | collective-permute-start | bytes 196616 | tf_op jit(solution)/shard_map/ppermute | solution.py:12
  42.7 20.4 %collective-permute-start.2 = (bf16[4,256,32]{1,2,0:T(8,128)(2,1)S(1)}, bf16[4,256,32]{1,2,0:T(8,128)(2,1)S(1)}, u32[]{:S(2)}, u32[]{:S(2)}) collective-permute-start(bf16[4,256,32]{1,2,0:T(8,128)(2,1)S(1)} %pad_maximum_fusion.8), channel_id=1, source_target_pairs={{0,508},{4,0},{8,4},{12,8},{16,12},{20,16},{24,20},{28,24},{32,28}... | collective-permute-start | bytes 196616 | tf_op jit(solution)/shard_map/ppermute | solution.py:12
  47.1 16.1 %collective-permute-start.1 = (bf16[4,256,32]{1,2,0:T(8,128)(2,1)S(1)}, bf16[4,256,32]{1,2,0:T(8,128)(2,1)S(1)}, u32[]{:S(2)}, u32[]{:S(2)}) collective-permute-start(bf16[4,256,32]{1,2,0:T(8,128)(2,1)S(1)} %pad_maximum_fusion.8), channel_id=1, source_target_pairs={{0,4},{4,8},{8,12},{12,16},{16,20},{20,24},{24,28},{28,32},{32,36}... | collective-permute-start | bytes 196616 | tf_op jit(solution)/shard_map/ppermute | solution.py:12
  49.0 14.3 %collective-permute-start = (bf16[4,256,32]{1,2,0:T(8,128)(2,1)S(1)}, bf16[4,256,32]{1,2,0:T(8,128)(2,1)S(1)}, u32[]{:S(2)}, u32[]{:S(2)}) collective-permute-start(bf16[4,256,32]{1,2,0:T(8,128)(2,1)S(1)} %pad_maximum_fusion.8), channel_id=1, source_target_pairs={{0,16},{4,20},{8,24},{12,28},{16,32},{20,36},{24,40},{28,44},{32,4... | collective-permute-start | bytes 196616 | tf_op jit(solution)/shard_map/ppermute | solution.py:12
  80.1 1.0 copy-start
  83.2 0.9 copy-start.5
  100.8 17.2 %collective-permute-start.7 = (bf16[4,256,16]{1,2,0:T(8,128)(2,1)S(1)}, bf16[4,256,16]{1,2,0:T(8,128)(2,1)S(1)}, u32[]{:S(2)}, u32[]{:S(2)}) collective-permute-start(bf16[4,256,16]{1,2,0:T(8,128)(2,1)S(1)} %pad_maximum_fusion.10), channel_id=1, source_target_pairs={{0,496},{4,500},{8,504},{12,508},{16,0},{20,4},{24,8},{28,12},{32,... | collective-permute-start | bytes 98312 | tf_op jit(solution)/shard_map/ppermute | solution.py:12
  107.2 10.9 %collective-permute-start.6 = (bf16[4,256,16]{1,2,0:T(8,128)(2,1)S(1)}, bf16[4,256,16]{1,2,0:T(8,128)(2,1)S(1)}, u32[]{:S(2)}, u32[]{:S(2)}) collective-permute-start(bf16[4,256,16]{1,2,0:T(8,128)(2,1)S(1)} %pad_maximum_fusion.10), channel_id=1, source_target_pairs={{0,508},{4,0},{8,4},{12,8},{16,12},{20,16},{24,20},{28,24},{32,28}... | collective-permute-start | bytes 98312 | tf_op jit(solution)/shard_map/ppermute | solution.py:12
  113.0 11.3 %collective-permute-start.5 = (bf16[4,256,16]{1,2,0:T(8,128)(2,1)S(1)}, bf16[4,256,16]{1,2,0:T(8,128)(2,1)S(1)}, u32[]{:S(2)}, u32[]{:S(2)}) collective-permute-start(bf16[4,256,16]{1,2,0:T(8,128)(2,1)S(1)} %pad_maximum_fusion.10), channel_id=1, source_target_pairs={{0,4},{4,8},{8,12},{12,16},{16,20},{20,24},{24,28},{28,32},{32,36}... | collective-permute-start | bytes 98312 | tf_op jit(solution)/shard_map/ppermute | solution.py:12
  114.9 9.5 %collective-permute-start.4 = (bf16[4,256,16]{1,2,0:T(8,128)(2,1)S(1)}, bf16[4,256,16]{1,2,0:T(8,128)(2,1)S(1)}, u32[]{:S(2)}, u32[]{:S(2)}) collective-permute-start(bf16[4,256,16]{1,2,0:T(8,128)(2,1)S(1)} %pad_maximum_fusion.10), channel_id=1, source_target_pairs={{0,16},{4,20},{8,24},{12,28},{16,32},{20,36},{24,40},{28,44},{32,4... | collective-permute-start | bytes 98312 | tf_op jit(solution)/shard_map/ppermute | solution.py:12
  127.5 5.6 %copy-start.2 = (bf16[9,64,256]{2,1,0:T(8,128)(2,1)S(1)}, bf16[9,64,256]{2,1,0:T(8,128)(2,1)}, u32[]{:S(2)}) copy-start(bf16[9,64,256]{2,1,0:T(8,128)(2,1)} %param.14) | copy-start | bytes 884740
  133.3 1.8 copy-start.6
  151.4 12.8 %collective-permute-start.11 = (bf16[4,256,16]{1,2,0:T(8,128)(2,1)S(1)}, bf16[4,256,16]{1,2,0:T(8,128)(2,1)S(1)}, u32[]{:S(2)}, u32[]{:S(2)}) collective-permute-start(bf16[4,256,16]{1,2,0:T(8,128)(2,1)S(1)} %pad_maximum_fusion.11), channel_id=1, source_target_pairs={{0,496},{4,500},{8,504},{12,508},{16,0},{20,4},{24,8},{28,12},{32,... | collective-permute-start | bytes 98312 | tf_op jit(solution)/shard_map/ppermute | solution.py:12
  153.4 11.0 %collective-permute-start.10 = (bf16[4,256,16]{1,2,0:T(8,128)(2,1)S(1)}, bf16[4,256,16]{1,2,0:T(8,128)(2,1)S(1)}, u32[]{:S(2)}, u32[]{:S(2)}) collective-permute-start(bf16[4,256,16]{1,2,0:T(8,128)(2,1)S(1)} %pad_maximum_fusion.11), channel_id=1, source_target_pairs={{0,508},{4,0},{8,4},{12,8},{16,12},{20,16},{24,20},{28,24},{32,28}... | collective-permute-start | bytes 98312 | tf_op jit(solution)/shard_map/ppermute | solution.py:12
  158.8 11.0 %collective-permute-start.9 = (bf16[4,256,16]{1,2,0:T(8,128)(2,1)S(1)}, bf16[4,256,16]{1,2,0:T(8,128)(2,1)S(1)}, u32[]{:S(2)}, u32[]{:S(2)}) collective-permute-start(bf16[4,256,16]{1,2,0:T(8,128)(2,1)S(1)} %pad_maximum_fusion.11), channel_id=1, source_target_pairs={{0,4},{4,8},{8,12},{12,16},{16,20},{20,24},{24,28},{28,32},{32,36}... | collective-permute-start | bytes 98312 | tf_op jit(solution)/shard_map/ppermute | solution.py:12
  160.7 9.2 %collective-permute-start.8 = (bf16[4,256,16]{1,2,0:T(8,128)(2,1)S(1)}, bf16[4,256,16]{1,2,0:T(8,128)(2,1)S(1)}, u32[]{:S(2)}, u32[]{:S(2)}) collective-permute-start(bf16[4,256,16]{1,2,0:T(8,128)(2,1)S(1)} %pad_maximum_fusion.11), channel_id=1, source_target_pairs={{0,16},{4,20},{8,24},{12,28},{16,32},{20,36},{24,40},{28,44},{32,4... | collective-permute-start | bytes 98312 | tf_op jit(solution)/shard_map/ppermute | solution.py:12
  173.0 5.6 %copy-start.3 = (bf16[9,64,256]{2,1,0:T(8,128)(2,1)S(1)}, bf16[9,64,256]{2,1,0:T(8,128)(2,1)}, u32[]{:S(2)}) copy-start(bf16[9,64,256]{2,1,0:T(8,128)(2,1)} %param.16) | copy-start | bytes 884740
  178.8 1.8 copy-start.7
  208.4 13.1 %collective-permute-start.15 = (bf16[4,256,32]{1,2,0:T(8,128)(2,1)S(1)}, bf16[4,256,32]{1,2,0:T(8,128)(2,1)S(1)}, u32[]{:S(2)}, u32[]{:S(2)}) collective-permute-start(bf16[4,256,32]{1,2,0:T(8,128)(2,1)S(1)} %pad_maximum_fusion.9), channel_id=1, source_target_pairs={{0,496},{4,500},{8,504},{12,508},{16,0},{20,4},{24,8},{28,12},{32,... | collective-permute-start | bytes 196616 | tf_op jit(solution)/shard_map/ppermute | solution.py:12
  210.3 11.3 %collective-permute-start.14 = (bf16[4,256,32]{1,2,0:T(8,128)(2,1)S(1)}, bf16[4,256,32]{1,2,0:T(8,128)(2,1)S(1)}, u32[]{:S(2)}, u32[]{:S(2)}) collective-permute-start(bf16[4,256,32]{1,2,0:T(8,128)(2,1)S(1)} %pad_maximum_fusion.9), channel_id=1, source_target_pairs={{0,508},{4,0},{8,4},{12,8},{16,12},{20,16},{24,20},{28,24},{32,28}... | collective-permute-start | bytes 196616 | tf_op jit(solution)/shard_map/ppermute | solution.py:12
  215.7 13.3 %collective-permute-start.13 = (bf16[4,256,32]{1,2,0:T(8,128)(2,1)S(1)}, bf16[4,256,32]{1,2,0:T(8,128)(2,1)S(1)}, u32[]{:S(2)}, u32[]{:S(2)}) collective-permute-start(bf16[4,256,32]{1,2,0:T(8,128)(2,1)S(1)} %pad_maximum_fusion.9), channel_id=1, source_target_pairs={{0,4},{4,8},{8,12},{12,16},{16,20},{20,24},{24,28},{28,32},{32,36}... | collective-permute-start | bytes 196616 | tf_op jit(solution)/shard_map/ppermute | solution.py:12
  217.7 11.5 %collective-permute-start.12 = (bf16[4,256,32]{1,2,0:T(8,128)(2,1)S(1)}, bf16[4,256,32]{1,2,0:T(8,128)(2,1)S(1)}, u32[]{:S(2)}, u32[]{:S(2)}) collective-permute-start(bf16[4,256,32]{1,2,0:T(8,128)(2,1)S(1)} %pad_maximum_fusion.9), channel_id=1, source_target_pairs={{0,16},{4,20},{8,24},{12,28},{16,32},{20,36},{24,40},{28,44},{32,4... | collective-permute-start | bytes 196616 | tf_op jit(solution)/shard_map/ppermute | solution.py:12
  242.6 3.6 %copy-start.1 = (bf16[9,64,256]{2,1,0:T(8,128)(2,1)S(1)}, bf16[9,64,256]{2,1,0:T(8,128)(2,1)}, u32[]{:S(2)}) copy-start(bf16[9,64,256]{2,1,0:T(8,128)(2,1)} %param.18) | copy-start | bytes 884740
  248.4 0.9 copy-start.8
where the time goes:
time: 256 us; the launch traced here: 251 us
  local copies, waits for them, and re-layouts  70.1 us (27%)
  starting transfers between devices  64.7 us (25%)
  blocking collectives  57.5 us (22%)
  other arithmetic  19.2 us (8%)
  waiting for transfers between devices  18.7 us (7%)
  between operations  11.4 us (4%)
  matrix products  8.95 us (3%)
    ppermute x16, starting transfers between devices, shifted(): lax.ppermute(array, axis, [(i, (i + by) % peers) for i in range(peers)])  64.7 us
    all_gather x4, blocking collectives, conv_block(): gathered = lax.all_gather(fields, 'chan', axis=0, tiled=True)  57.5 us
    unnamed x35, local copies, waits for them, and re-layouts  21.7 us
    ppermute x16, waiting for transfers between devices, shifted(): lax.ppermute(array, axis, [(i, (i + by) % peers) for i in range(peers)])  18.7 us
    concatenate x4, other arithmetic, with_rims(): jnp.concatenate([west_rim[:, :, None], fields, east_rim[:, :, None]], axi...  17.4 us
    broadcast_in_dim x4, local copies, waits for them, and re-layouts, with_rims(): east_rim[:, :, None]  11.6 us
    concatenate x4, local copies, waits for them, and re-layouts, with_rims(): jnp.concatenate([west_rim[:, :, None], fields, east_rim[:, :, None]], axi...  11.1 us
    broadcast_in_dim x4, local copies, waits for them, and re-layouts, with_rims(): west_rim[:, :, None]  9.81 us
  transfers between devices with their start and end apart: 16, of which 3 were waited for; matrix products, arithmetic and copies ran while one was open for 1% of the time, Pallas kernels for 0%

commit v1 on v0

v1 whole, which is shorter than its diff:
```python
import functools

import jax
import jax.numpy as jnp
from jax import lax
from jax.experimental import pallas as pl
from jax.experimental.pallas import tpu as pltpu
from jax.sharding import PartitionSpec as P

TILE_COLS = 4
CB = 64
PEERS = 4
C = CB * PEERS
S1 = 32
S2 = 16
Q = 4
QW = S1 * S1 // Q
GELU_A = 0.7978845608028654
GELU_B = 0.044715
MESH = pl.DeviceIdType.MESH
F32 = jnp.float32
BF16 = jnp.bfloat16


def iota(shape, dim):
    return lax.broadcasted_iota(jnp.int32, shape, dim)


def gelu(v):
    return 0.5 * v * (1.0 + jnp.tanh(GELU_A * (v + GELU_B * (v * v * v))))


def dot(a, b):
    return lax.dot_general(a, b, (((1,), (0,)), ((), ())), preferred_element_type=F32)


def dot_t(a, b):
    return lax.dot_general(a, b, (((1,), (1,)), ((), ())), preferred_element_type=F32)


def one_hot(cond):
    return jnp.where(cond, 1.0, 0.0).astype(BF16)


def edge_position(edge, along, side):
    return jnp.where(
        edge == 0,
        along,
        jnp.where(
            edge == 1,
            (side - 1) * side + along,
            jnp.where(edge == 2, along * side, along * side + side - 1),
        ),
    )


def kernel(
    tiles,
    codes,
    x_hbm,
    w0_hbm,
    w1_hbm,
    w2_hbm,
    w3_hbm,
    b0_hbm,
    b1_hbm,
    b2_hbm,
    b3_hbm,
    out_ref,
    g1,
    g2,
    g3,
    g4,
    enc,
    w_v,
    b_v,
    bias_v,
    sel1,
    sel2,
    exp1,
    exp2,
    pool,
    sb,
    rb,
    taps,
    x_sem,
    w_sem,
    b_sem,
    fine_send,
    fine_recv,
    coarse_send,
    coarse_recv,
    rim_send,
    rim_recv,
):
    tile = lax.axis_index("face")
    chan = lax.axis_index("chan")
    partner = chan + 1 - 2 * (chan % 2)
    across = (chan + 2) % 4
    diagonal = (partner + 2) % 4
    near = [
        (tile + TILE_COLS) % tiles,
        (tile + tiles - TILE_COLS) % tiles,
        (tile + 1) % tiles,
        (tile + tiles - 1) % tiles,
    ]
    mine = pl.ds(pl.multiple_of(chan * CB, CB), CB)
    across_rows = pl.ds(pl.multiple_of(across * CB, CB), CB)

    x_copies = [
        pltpu.make_async_copy(x_hbm.at[:, pl.ds(q * QW, QW)], g1.at[q, mine, :], x_sem.at[q])
        for q in range(Q)
    ]
    for copy in x_copies:
        copy.start()
    w_copies = []
    b_copies = []
    for i, w in enumerate((w0_hbm, w1_hbm, w2_hbm, w3_hbm)):
        w_copies.append(pltpu.make_async_copy(w, w_v.at[i], w_sem.at[i]))
    for i, b in enumerate((b0_hbm, b1_hbm, b2_hbm, b3_hbm)):
        b_copies.append(pltpu.make_async_copy(b, b_v.at[i], b_sem.at[i]))
    for copy in w_copies + b_copies:
        copy.start()

    barrier = pltpu.get_barrier_semaphore()
    for peer in (partner, across, diagonal):
        pl.semaphore_signal(barrier, inc=1, device_id=(tile, peer), device_id_type=MESH)
    for side in range(4):
        for step in range(PEERS):
            peer = (chan + step) % PEERS
            pl.semaphore_signal(
                barrier, inc=1, device_id=(near[side], peer), device_id_type=MESH
            )

    lane = iota((1, 128), 1)
    slot = lane // 32
    along = lane % 32
    codes_here = [codes[side, near[side]] for side in range(4)]
    code = jnp.where(
        slot == 0,
        codes_here[0],
        jnp.where(slot == 1, codes_here[1], jnp.where(slot == 2, codes_here[2], codes_here[3])),
    )
    edge = code % 4
    for size, sel in ((S1, sel1), (S2, sel2)):
        place = jnp.where(code >= 4, size - 1 - along, along)
        cell = jnp.where(along < size, edge_position(edge, place, size), -1)
        sel[...] = one_hot(iota((size * size, 128), 0) == cell)
    row = iota((128, 1), 0)
    for size, exp in ((S1, exp1), (S2, exp2)):
        cell = jnp.where(
            row % 32 < size, edge_position(row // 32, row % 32, size), -1
        )
        exp[...] = one_hot(iota((128, size * size), 1) == cell)
    cell = iota((QW, QW), 0)
    pool[...] = one_hot(
        (cell // S1 // 2) * S2 + (cell % S1) // 2 == iota((QW, QW), 1) % (QW // 4)
    )
    eye = iota((CB, CB), 0) == iota((CB, CB), 1)
    for copy in b_copies:
        copy.wait()
    for i in range(4):
        column = jnp.sum(
            jnp.where(eye, jnp.broadcast_to(b_v[i], (CB, CB)), 0.0), axis=1, keepdims=True
        )
        bias_v[i] = jnp.broadcast_to(column, (CB, 128))

    def pack_rims(layer, picked):
        for side in range(4):
            block = None
            for group in range(4):
                part = picked[16 * group : 16 * group + 16, :]
                shift = (32 * (group - side)) % 128
                if shift:
                    part = pltpu.roll(part, shift, 1)
                block = part if block is None else jnp.where(slot == group, part, block)
            sb[layer, side] = block.astype(BF16)

    def rim_copies(layer):
        copies = []
        for step in range(PEERS):
            for side in range(4):
                peer = (chan + step) % PEERS
                copies.append(
                    pltpu.make_async_remote_copy(
                        src_ref=sb.at[layer, side],
                        dst_ref=rb.at[layer, chan, side],
                        send_sem=rim_send.at[layer, step, side],
                        recv_sem=rim_recv.at[layer, step, side],
                        device_id=(near[side], peer),
                        device_id_type=MESH,
                    )
                )
        return copies

    def fine_copies(index, g):
        def copies_to(kind, peer, rows):
            return [
                pltpu.make_async_remote_copy(
                    src_ref=g.at[q, rows, :],
                    dst_ref=g.at[q, rows, :],
                    send_sem=fine_send.at[index, kind, q],
                    recv_sem=fine_recv.at[index, kind, q],
                    device_id=(tile, peer),
                    device_id_type=MESH,
                )
                for q in range(Q)
            ]

        return (
            copies_to(0, partner, mine),
            copies_to(1, across, mine),
            copies_to(2, partner, across_rows),
        )

    def coarse_copies(index, g):
        return [
            pltpu.make_async_remote_copy(
                src_ref=g.at[mine, :],
                dst_ref=g.at[mine, :],
                send_sem=coarse_send.at[index, kind],
                recv_sem=coarse_recv.at[index, kind],
                device_id=(tile, peer),
                device_id_type=MESH,
            )
            for kind, peer in enumerate((across, diagonal, partner))
        ]

    def rim_sums(layer, size, exp):
        blocks = []
        for source in range(PEERS):
            parts = [rb[layer, source, side].astype(F32) for side in range(4)]
            for group in range(4):
                block = None
                for side in range(4):
                    part = parts[side]
                    shift = (32 * (side - group)) % 128
                    if shift:
                        part = pltpu.roll(part, shift, 1)
                    block = part if block is None else jnp.where(slot == side, part, block)
                blocks.append(block.astype(BF16))
        rims = jnp.concatenate(blocks, axis=0)
        r = dot(w_v[layer].reshape(9 * CB, C), rims)
        r = [r[CB * t : CB * t + CB, :] for t in range(9)]

        def by_side(north, south, west, east):
            return jnp.where(
                slot == 0,
                r[north],
                jnp.where(slot == 1, r[south], jnp.where(slot == 2, r[west], r[east])),
            )

        before = jnp.where(along == 0, 0.0, pltpu.roll(by_side(0, 6, 0, 2), 1, 1))
        after = jnp.where(along == size - 1, 0.0, pltpu.roll(by_side(2, 8, 6, 8), 127, 1))
        total = before + by_side(1, 7, 3, 5) + after
        high = total.astype(BF16)
        low = (total - high.astype(F32)).astype(BF16)
        spread = dot(jnp.concatenate([high, low], axis=0), exp[...])
        return spread[:CB] + spread[CB:]

    def conv_rows(layer, size, rows, rims):
        cells = size * size
        place = iota((1, cells), 1)
        column = place % size
        sums = []
        for dx in range(3):
            t = [taps[pl.ds(CB * (3 * dy + dx) + rows, 16), :cells] for dy in range(3)]
            above = jnp.where(place >= size, pltpu.roll(t[0], size, 1), 0.0)
            below = jnp.where(place < cells - size, pltpu.roll(t[2], cells - size, 1), 0.0)
            sums.append(t[1] + (above + below))
        left = jnp.where(column == 0, 0.0, pltpu.roll(sums[0], 1, 1))
        right = jnp.where(column == size - 1, 0.0, pltpu.roll(sums[2], cells - 1, 1))
        bias = bias_v[layer, rows : rows + 16, 0:1]
        return (sums[1] + (left + right)) + (rims[rows : rows + 16, :] + bias)

    for copy in x_copies:
        copy.wait()
    picked = sum(dot(g1[q, mine, :], sel1[QW * q : QW * q + QW, :]) for q in range(Q))
    pack_rims(0, picked)

    pl.semaphore_wait(barrier, 3 + 4 * PEERS)

    sent = []
    rims0 = rim_copies(0)
    to_partner, to_across, relay = fine_copies(0, g1)
    for q in range(Q):
        to_across[q].start()
    for copy in rims0:
        copy.start()
    for q in range(Q):
        to_partner[q].start()
    for q in range(Q):
        to_across[q].wait_recv()
        relay[q].start()
    w_copies[0].wait()
    for q in range(Q):
        to_partner[q].wait_recv()
        relay[q].wait_recv()
        taps[:, QW * q : QW * q + QW] = dot(w_v[0].reshape(9 * CB, C), g1[q])
    for copy in rims0:
        copy.wait_recv()
    sent += rims0 + to_partner + to_across + relay
    rims = rim_sums(0, S1, exp1)
    for rows in range(0, CB, 16):
        act = gelu(conv_rows(0, S1, rows, rims))
        own = pl.ds(pl.multiple_of(chan * CB + rows, 16), 16)
        for q in range(Q):
            field = g1[q, own, :].astype(F32)
            enc[q, rows : rows + 16, :] = (field + act[:, QW * q : QW * q + QW]).astype(BF16)

    group = iota((1, QW), 1) // (QW // 4)
    pooled = dot(enc[...].reshape(Q * CB, QW), pool[...])
    coarse = pooled[:CB]
    for q in range(1, Q):
        coarse = jnp.where(group == q, pooled[CB * q : CB * q + CB], coarse)
    coarse = (coarse * 0.25).astype(BF16)
    middle = coarse
    for layer, g in ((1, g2), (2, g3)):
        g[mine, :] = middle
        pack_rims(layer, dot(middle, sel2[...]))
        rims_l = rim_copies(layer)
        copies = coarse_copies(layer - 1, g)
        for copy in rims_l:
            copy.start()
        for copy in copies:
            copy.start()
        w_copies[layer].wait()
        for copy in copies:
            copy.wait_recv()
        taps[:, :QW] = dot(w_v[layer].reshape(9 * CB, C), g[...])
        for copy in rims_l:
            copy.wait_recv()
        sent += rims_l + copies
        rims = rim_sums(layer, S2, exp2)
        parts = []
        for rows in range(0, CB, 16):
            act = gelu(conv_rows(layer, S2, rows, rims))
            parts.append((middle[rows : rows + 16, :].astype(F32) + act).astype(BF16))
        middle = jnp.concatenate(parts, axis=0)

    spread = jnp.concatenate(
        [jnp.where(group == q, middle.astype(F32), 0.0).astype(BF16) for q in range(Q)], axis=0
    )
    refined = dot_t(spread, pool[...])
    picked = None
    for q in range(Q):
        joined = (refined[CB * q : CB * q + CB] + enc[q].astype(F32)).astype(BF16)
        g4[q, mine, :] = joined
        part = dot(joined, sel1[QW * q : QW * q + QW, :])
        picked = part if picked is None else picked + part
    pack_rims(3, picked)
    rims3 = rim_copies(3)
    to_partner, to_across, relay = fine_copies(1, g4)
    for copy in rims3:
        copy.start()
    for q in range(Q):
        to_across[q].start()
    for q in range(Q):
        to_partner[q].start()
    for q in range(Q):
        to_across[q].wait_recv()
        relay[q].start()
    w_copies[3].wait()
    for q in range(Q):
        to_partner[q].wait_recv()
        relay[q].wait_recv()
        taps[:, QW * q : QW * q + QW] = dot(w_v[3].reshape(9 * CB, C), g4[q])
    for copy in rims3:
        copy.wait_recv()
    sent += rims3 + to_partner + to_across + relay
    rims = rim_sums(3, S1, exp1)
    for rows in range(0, CB, 16):
        act = gelu(conv_rows(3, S1, rows, rims))
        own = pl.ds(pl.multiple_of(chan * CB + rows, 16), 16)
        for q in range(Q):
            field = g4[q, own, :].astype(F32)
            out_ref[rows : rows + 16, QW * q : QW * q + QW] = (
                field + act[:, QW * q : QW * q + QW]
            ).astype(BF16)
    for copy in sent:
        copy.wait_send()


def on_device(
    tiles,
    field_in,
    edge_codes,
    weight_enc,
    bias_enc,
    weight_mid_a,
    bias_mid_a,
    weight_mid_b,
    bias_mid_b,
    weight_dec,
    bias_dec,
):
    hbm = pl.BlockSpec(memory_space=pltpu.MemorySpace.HBM)
    vmem = pl.BlockSpec(memory_space=pltpu.MemorySpace.VMEM)
    dma = pltpu.SemaphoreType.DMA
    biases = [b.reshape(1, CB) for b in (bias_enc, bias_mid_a, bias_mid_b, bias_dec)]
    return pl.pallas_call(
        functools.partial(kernel, tiles),
        out_shape=jax.ShapeDtypeStruct((CB, S1 * S1), BF16),
        in_specs=[pl.BlockSpec(memory_space=pltpu.MemorySpace.SMEM)] + [hbm] * 9,
        out_specs=vmem,
        scratch_shapes=[
            pltpu.VMEM((Q, C, QW), BF16),
            pltpu.VMEM((C, QW), BF16),
            pltpu.VMEM((C, QW), BF16),
            pltpu.VMEM((Q, C, QW), BF16),
            pltpu.VMEM((Q, CB, QW), BF16),
            pltpu.VMEM((4, 9, CB, C), BF16),
            pltpu.VMEM((4, 1, CB), F32),
            pltpu.VMEM((4, CB, 128), F32),
            pltpu.VMEM((S1 * S1, 128), BF16),
            pltpu.VMEM((S2 * S2, 128), BF16),
            pltpu.VMEM((128, S1 * S1), BF16),
            pltpu.VMEM((128, S2 * S2), BF16),
            pltpu.VMEM((QW, QW), BF16),
            pltpu.VMEM((4, 4, 16, 128), BF16),
            pltpu.VMEM((4, PEERS, 4, 16, 128), BF16),
            pltpu.VMEM((9 * CB, S1 * S1), F32),
            dma((Q,)),
            dma((4,)),
            dma((4,)),
            dma((2, 3, Q)),
            dma((2, 3, Q)),
            dma((2, 3)),
            dma((2, 3)),
            dma((4, PEERS, 4)),
            dma((4, PEERS, 4)),
        ],
        compiler_params=pltpu.CompilerParams(
            collective_id=0, has_side_effects=True, vmem_limit_bytes=62 * 1024 * 1024
        ),
        name="unet_window",
    )(
        edge_codes.T,
        field_in,
        weight_enc,
        weight_mid_a,
        weight_mid_b,
        weight_dec,
        *biases,
    )


def solution(mesh):
    weights = P(None, "chan", None)
    in_specs = (
        P("chan", "face"),
        P(),
        weights,
        P("chan"),
        weights,
        P("chan"),
        weights,
        P("chan"),
        weights,
        P("chan"),
    )
    return jax.shard_map(
        functools.partial(on_device, mesh.shape["face"]),
        mesh=mesh,
        in_specs=in_specs,
        out_specs=P("chan", "face"),
        check_vma=False,
    )
```

time: 256 us -> 55.7 us (0.22); the launches traced: 251 us -> 55.5 us
  local copies, waits for them, and re-layouts: 70.1 us -> 1.57 us
  starting transfers between devices: 64.7 us -> 0 us
  blocking collectives: 57.5 us -> 0 us
  Pallas kernels: 0 us -> 53.9 us
  other arithmetic: 19.2 us -> 0 us
  waiting for transfers between devices: 18.7 us -> 0 us
  between operations: 11.4 us -> 0.01 us
  matrix products: 8.95 us -> 0 us
    ppermute x16 -> x0, starting transfers between devices: 64.7 us -> none  [shifted(): lax.ppermute(array, axis, [(i, (i + by) % peers) for i in range(peers)])]
    all_gather x4 -> x0, blocking collectives: 57.5 us -> none  [conv_block(): gathered = lax.all_gather(fields, 'chan', axis=0, tiled=True)]
    pallas_call x0 -> x1, Pallas kernels: none -> 53.9 us  [on_device(): pl.pallas_call(functools.partial(kernel, tiles), out_shape=jax.ShapeDtype...]
    broadcast_in_dim x17 -> x0, local copies, waits for them, and re-layouts: 21.7 us -> none  [the longest x4 11.6 us: with_rims(): east_rim[:, :, None]]
    unnamed x35 -> x1, local copies, waits for them, and re-layouts: 21.7 us -> 1.57 us
    ppermute x16 -> x0, waiting for transfers between devices: 18.7 us -> none  [shifted(): lax.ppermute(array, axis, [(i, (i + by) % peers) for i in range(peers)])]
    concatenate x8 -> x0, other arithmetic: 17.7 us -> none  [the longest x4 17.4 us: with_rims(): jnp.concatenate([west_rim[:, :, None], fields, east_rim[:, :, None]], axi...]
    concatenate x4 -> x0, local copies, waits for them, and re-layouts: 11.1 us -> none  [with_rims(): jnp.concatenate([west_rim[:, :, None], fields, east_rim[:, :, None]], axi...]
  transfers between devices with their start and end apart: 16 -> 0, of which waited for: 3 -> 0; matrix products, arithmetic and copies ran while one was open for 1% -> 0% of each run, Pallas kernels for 0% -> 0%
where the time goes in v1:
time: 55.7 us; the launch traced here: 55.5 us
  Pallas kernels  53.9 us (97%)
  local copies, waits for them, and re-layouts  1.57 us (3%)
    pallas_call x1, Pallas kernels, on_device(): pl.pallas_call(functools.partial(kernel, tiles), out_shape=jax.ShapeDtype...  53.9 us
    unnamed x1, local copies, waits for them, and re-layouts  1.57 us

profile of v1, /device:TPU:1, one launch (start us, length us, event | category | flops | bytes accessed | tf_op | source)
XLA Modules:
  0.0 55.5 jit_solution(16147958885901878129)
XLA Ops:
  0.0 53.9 %unet_window.1 = bf16[64,1024]{1,0:T(8,128)(2,1)} custom-call(s32[4,128]{1,0:T(4,128)} %bitcast.5, bf16[64,1024]{1,0:T(8,128)(2,1)} %x_hbm.1, bf16[9,64,256]{2,1,0:T(8,128)(2,1)} %w0_hbm.1, bf16[9,64,256]{2,1,0:T(8,128)(2,1)} %w1_hbm.1, bf16[9,64,256]{2,1,0:T(8,128)(2,1)} %w2_hbm.1, bf16[9,64,256]{2,1,0:T(8,128)(2,1)} %w3_hbm.1, f32[1,64]{1,0:T(1,128)} %bitcast.6, ...), custom_call_target="tpu_custom_call" | custom-call | tf_op jit(solution)/shard_map/unet_window/pallas_call | solution.py:401
  53.9 1.6 %copy.12 = bf16[64,1024]{1,0:T(8,128)(2,1)} copy(bf16[64,1024]{1,0:T(8,128)(2,1)} %unet_window.1) | data formatting | bytes 262144

commit v2 on v1

--- a/solution.py
+++ b/solution.py
@@ -56,7 +56,7 @@
 
 def kernel(
     tiles,
-    codes,
+    codes_hbm,
     x_hbm,
     w0_hbm,
     w1_hbm,
@@ -67,11 +67,13 @@
     b2_hbm,
     b3_hbm,
     out_ref,
+    codes,
     g1,
     g2,
     g3,
     g4,
-    enc,
+    g5,
+    joined,
     w_v,
     b_v,
     bias_v,
@@ -80,13 +82,16 @@
     exp1,
     exp2,
     pool,
+    up,
     sb,
     rb,
     taps,
+    codes_sem,
     x_sem,
     w_sem,
     b_sem,
     fine_send,
+    partner_recv,
     fine_recv,
     coarse_send,
     coarse_recv,
@@ -107,21 +112,6 @@
     mine = pl.ds(pl.multiple_of(chan * CB, CB), CB)
     across_rows = pl.ds(pl.multiple_of(across * CB, CB), CB)
 
-    x_copies = [
-        pltpu.make_async_copy(x_hbm.at[:, pl.ds(q * QW, QW)], g1.at[q, mine, :], x_sem.at[q])
-        for q in range(Q)
-    ]
-    for copy in x_copies:
-        copy.start()
-    w_copies = []
-    b_copies = []
-    for i, w in enumerate((w0_hbm, w1_hbm, w2_hbm, w3_hbm)):
-        w_copies.append(pltpu.make_async_copy(w, w_v.at[i], w_sem.at[i]))
-    for i, b in enumerate((b0_hbm, b1_hbm, b2_hbm, b3_hbm)):
-        b_copies.append(pltpu.make_async_copy(b, b_v.at[i], b_sem.at[i]))
-    for copy in w_copies + b_copies:
-        copy.start()
-
     barrier = pltpu.get_barrier_semaphore()
     for peer in (partner, across, diagonal):
         pl.semaphore_signal(barrier, inc=1, device_id=(tile, peer), device_id_type=MESH)
@@ -132,38 +122,56 @@
                 barrier, inc=1, device_id=(near[side], peer), device_id_type=MESH
             )
 
+    codes_copy = pltpu.make_async_copy(codes_hbm, codes, codes_sem)
+    codes_copy.start()
+    x_copies = [
+        pltpu.make_async_copy(x_hbm.at[:, pl.ds(q * QW, QW)], g1.at[q, mine, :], x_sem)
+        for q in range(Q)
+    ]
+    for copy in x_copies:
+        copy.start()
+    w_copies = []
+    b_copies = []
+    for i, w in enumerate((w0_hbm, w1_hbm, w2_hbm, w3_hbm)):
+        w_copies.append(pltpu.make_async_copy(w, w_v.at[i], w_sem.at[i]))
+    for i, b in enumerate((b0_hbm, b1_hbm, b2_hbm, b3_hbm)):
+        b_copies.append(pltpu.make_async_copy(b, b_v.at[i], b_sem.at[i]))
+
     lane = iota((1, 128), 1)
     slot = lane // 32
     along = lane % 32
-    codes_here = [codes[side, near[side]] for side in range(4)]
-    code = jnp.where(
-        slot == 0,
-        codes_here[0],
-        jnp.where(slot == 1, codes_here[1], jnp.where(slot == 2, codes_here[2], codes_here[3])),
-    )
-    edge = code % 4
-    for size, sel in ((S1, sel1), (S2, sel2)):
+
+    def wait_bytes(ref, sem):
+        pltpu.make_async_copy(ref, ref, sem).wait()
+
+    def pick_table(code, size, sel):
         place = jnp.where(code >= 4, size - 1 - along, along)
-        cell = jnp.where(along < size, edge_position(edge, place, size), -1)
+        cell = jnp.where(along < size, edge_position(code % 4, place, size), -1)
         sel[...] = one_hot(iota((size * size, 128), 0) == cell)
-    row = iota((128, 1), 0)
-    for size, exp in ((S1, exp1), (S2, exp2)):
-        cell = jnp.where(
-            row % 32 < size, edge_position(row // 32, row % 32, size), -1
+
+    def other_tables():
+        row = iota((128, 1), 0)
+        for size, exp in ((S1, exp1), (S2, exp2)):
+            cell = jnp.where(
+                row % 32 < size, edge_position(row // 32, row % 32, size), -1
+            )
+            exp[...] = one_hot(iota((128, size * size), 1) == cell)
+        cell = iota((QW, QW), 0)
+        pool[...] = one_hot(
+            (cell // S1 // 2) * S2 + (cell % S1) // 2 == iota((QW, QW), 1) % (QW // 4)
         )
-        exp[...] = one_hot(iota((128, size * size), 1) == cell)
-    cell = iota((QW, QW), 0)
-    pool[...] = one_hot(
-        (cell // S1 // 2) * S2 + (cell % S1) // 2 == iota((QW, QW), 1) % (QW // 4)
-    )
-    eye = iota((CB, CB), 0) == iota((CB, CB), 1)
-    for copy in b_copies:
-        copy.wait()
-    for i in range(4):
-        column = jnp.sum(
-            jnp.where(eye, jnp.broadcast_to(b_v[i], (CB, CB)), 0.0), axis=1, keepdims=True
-        )
-        bias_v[i] = jnp.broadcast_to(column, (CB, 128))
+        cell = iota((1, QW), 1)
+        cell = (cell // S1 // 2) * S2 + (cell % S1) // 2
+        for q in range(Q):
+            up[q] = one_hot(iota((QW, QW), 0) == cell + q * (QW // 4))
+        eye = iota((CB, CB), 0) == iota((CB, CB), 1)
+        for copy in b_copies:
+            copy.wait()
+        for i in range(4):
+            column = jnp.sum(
+                jnp.where(eye, jnp.broadcast_to(b_v[i], (CB, CB)), 0.0), axis=1, keepdims=True
+            )
+            bias_v[i] = jnp.broadcast_to(column, (CB, 128))
 
     def pack_rims(layer, picked):
         for side in range(4):
@@ -185,22 +193,22 @@
                     pltpu.make_async_remote_copy(
                         src_ref=sb.at[layer, side],
                         dst_ref=rb.at[layer, chan, side],
-                        send_sem=rim_send.at[layer, step, side],
-                        recv_sem=rim_recv.at[layer, step, side],
+                        send_sem=rim_send.at[layer],
+                        recv_sem=rim_recv.at[layer],
                         device_id=(near[side], peer),
                         device_id_type=MESH,
                     )
                 )
         return copies
 
-    def fine_copies(index, g):
-        def copies_to(kind, peer, rows):
+    def fine_copies(index, g, source):
+        def copies_to(kind, peer, rows, source, recv):
             return [
                 pltpu.make_async_remote_copy(
-                    src_ref=g.at[q, rows, :],
+                    src_ref=source(q),
                     dst_ref=g.at[q, rows, :],
-                    send_sem=fine_send.at[index, kind, q],
-                    recv_sem=fine_recv.at[index, kind, q],
+                    send_sem=fine_send.at[index, kind],
+                    recv_sem=recv[q],
                     device_id=(tile, peer),
                     device_id_type=MESH,
                 )
@@ -208,9 +216,15 @@
             ]
 
         return (
-            copies_to(0, partner, mine),
-            copies_to(1, across, mine),
-            copies_to(2, partner, across_rows),
+            copies_to(0, partner, mine, source, [partner_recv.at[index]] * Q),
+            copies_to(1, across, mine, source, [fine_recv.at[index, 0, q] for q in range(Q)]),
+            copies_to(
+                2,
+                partner,
+                across_rows,
+                lambda q: g.at[q, across_rows, :],
+                [fine_recv.at[index, 1, q] for q in range(Q)],
+            ),
         )
 
     def coarse_copies(index, g):
@@ -218,13 +232,16 @@
             pltpu.make_async_remote_copy(
                 src_ref=g.at[mine, :],
                 dst_ref=g.at[mine, :],
-                send_sem=coarse_send.at[index, kind],
-                recv_sem=coarse_recv.at[index, kind],
+                send_sem=coarse_send.at[index],
+                recv_sem=coarse_recv.at[index],
                 device_id=(tile, peer),
                 device_id_type=MESH,
             )
-            for kind, peer in enumerate((across, diagonal, partner))
+            for peer in (across, diagonal, partner)
         ]
+
+    def coarse_wait(g, sem):
+        wait_bytes(g.at[pl.ds(0, 3 * CB), :], sem)
 
     def rim_sums(layer, size, exp):
         blocks = []
@@ -273,43 +290,47 @@
         bias = bias_v[layer, rows : rows + 16, 0:1]
         return (sums[1] + (left + right)) + (rims[rows : rows + 16, :] + bias)
 
-    for copy in x_copies:
-        copy.wait()
+    to_partner, to_across, relay = fine_copies(0, g1, lambda q: x_hbm.at[:, pl.ds(q * QW, QW)])
+    pl.semaphore_wait(barrier, 3 + 4 * PEERS)
+    for copy in to_across + to_partner:
+        copy.start()
+    for copy in b_copies + w_copies:
+        copy.start()
+    codes_copy.wait()
+    codes_here = [codes[side, near[side]] for side in range(4)]
+    code = jnp.where(
+        slot == 0,
+        codes_here[0],
+        jnp.where(slot == 1, codes_here[1], jnp.where(slot == 2, codes_here[2], codes_here[3])),
+    )
+    pick_table(code, S1, sel1)
+    wait_bytes(g1.at[:, mine, :], x_sem)
     picked = sum(dot(g1[q, mine, :], sel1[QW * q : QW * q + QW, :]) for q in range(Q))
     pack_rims(0, picked)
-
-    pl.semaphore_wait(barrier, 3 + 4 * PEERS)
-
-    sent = []
-    rims0 = rim_copies(0)
-    to_partner, to_across, relay = fine_copies(0, g1)
-    for q in range(Q):
-        to_across[q].start()
-    for copy in rims0:
-        copy.start()
-    for q in range(Q):
-        to_partner[q].start()
+    for copy in rim_copies(0):
+        copy.start()
+    pick_table(code, S2, sel2)
+    other_tables()
+    w_copies[0].wait()
     for q in range(Q):
         to_across[q].wait_recv()
         relay[q].start()
-    w_copies[0].wait()
+    wait_bytes(g1.at[:, mine, :], partner_recv.at[0])
     for q in range(Q):
-        to_partner[q].wait_recv()
         relay[q].wait_recv()
         taps[:, QW * q : QW * q + QW] = dot(w_v[0].reshape(9 * CB, C), g1[q])
-    for copy in rims0:
-        copy.wait_recv()
-    sent += rims0 + to_partner + to_across + relay
+    wait_bytes(rb.at[0], rim_recv.at[0])
     rims = rim_sums(0, S1, exp1)
     for rows in range(0, CB, 16):
         act = gelu(conv_rows(0, S1, rows, rims))
         own = pl.ds(pl.multiple_of(chan * CB + rows, 16), 16)
         for q in range(Q):
             field = g1[q, own, :].astype(F32)
-            enc[q, rows : rows + 16, :] = (field + act[:, QW * q : QW * q + QW]).astype(BF16)
-
+            g4[q, own, :] = (field + act[:, QW * q : QW * q + QW]).astype(BF16)
+
+    to_partner, to_across, relay = fine_copies(1, g4, lambda q: g4.at[q, mine, :])
     group = iota((1, QW), 1) // (QW // 4)
-    pooled = dot(enc[...].reshape(Q * CB, QW), pool[...])
+    pooled = dot(g4[:, mine, :].reshape(Q * CB, QW), pool[...])
     coarse = pooled[:CB]
     for q in range(1, Q):
         coarse = jnp.where(group == q, pooled[CB * q : CB * q + CB], coarse)
@@ -317,20 +338,25 @@
     middle = coarse
     for layer, g in ((1, g2), (2, g3)):
         g[mine, :] = middle
+        for copy in coarse_copies(layer - 1, g):
+            copy.start()
         pack_rims(layer, dot(middle, sel2[...]))
-        rims_l = rim_copies(layer)
-        copies = coarse_copies(layer - 1, g)
-        for copy in rims_l:
+        for copy in rim_copies(layer):
             copy.start()
-        for copy in copies:
-            copy.start()
+        if layer == 1:
+            for copy in to_across[: Q // 2] + to_partner:
+                copy.start()
         w_copies[layer].wait()
-        for copy in copies:
-            copy.wait_recv()
+        coarse_wait(g, coarse_recv.at[layer - 1])
         taps[:, :QW] = dot(w_v[layer].reshape(9 * CB, C), g[...])
-        for copy in rims_l:
-            copy.wait_recv()
-        sent += rims_l + copies
+        wait_bytes(rb.at[layer], rim_recv.at[layer])
+        if layer == 1:
+            for copy in to_across[Q // 2 :]:
+                copy.start()
+        half = range(Q // 2 * (layer - 1), Q // 2 * layer)
+        for q in half:
+            to_across[q].wait_recv()
+            relay[q].start()
         rims = rim_sums(layer, S2, exp2)
         parts = []
         for rows in range(0, CB, 16):
@@ -338,47 +364,44 @@
             parts.append((middle[rows : rows + 16, :].astype(F32) + act).astype(BF16))
         middle = jnp.concatenate(parts, axis=0)
 
-    spread = jnp.concatenate(
-        [jnp.where(group == q, middle.astype(F32), 0.0).astype(BF16) for q in range(Q)], axis=0
-    )
-    refined = dot_t(spread, pool[...])
+    g5[mine, :] = middle
+    for copy in coarse_copies(2, g5):
+        copy.start()
     picked = None
     for q in range(Q):
-        joined = (refined[CB * q : CB * q + CB] + enc[q].astype(F32)).astype(BF16)
-        g4[q, mine, :] = joined
-        part = dot(joined, sel1[QW * q : QW * q + QW, :])
+        own = (dot(middle, up[q]) + g4[q, mine, :].astype(F32)).astype(BF16)
+        part = dot(own, sel1[QW * q : QW * q + QW, :])
         picked = part if picked is None else picked + part
     pack_rims(3, picked)
-    rims3 = rim_copies(3)
-    to_partner, to_across, relay = fine_copies(1, g4)
-    for copy in rims3:
-        copy.start()
+    for copy in rim_copies(3):
+        copy.start()
+    w_copies[3].wait()
+    wait_bytes(g4.at[:, mine, :], partner_recv.at[1])
     for q in range(Q):
-        to_across[q].start()
+        relay[q].wait_recv()
+    for index in range(2):
+        for kind in range(3):
+            wait_bytes(g4.at[:, mine, :], fine_send.at[index, kind])
+    for layer in range(3):
+        wait_bytes(rb.at[layer], rim_send.at[layer])
+    for index in range(2):
+        coarse_wait(g2, coarse_send.at[index])
+    coarse_wait(g5, coarse_recv.at[2])
     for q in range(Q):
-        to_partner[q].start()
-    for q in range(Q):
-        to_across[q].wait_recv()
-        relay[q].start()
-    w_copies[3].wait()
-    for q in range(Q):
-        to_partner[q].wait_recv()
-        relay[q].wait_recv()
-        taps[:, QW * q : QW * q + QW] = dot(w_v[3].reshape(9 * CB, C), g4[q])
-    for copy in rims3:
-        copy.wait_recv()
-    sent += rims3 + to_partner + to_across + relay
+        joined[q] = (dot(g5[...], up[q]) + g4[q].astype(F32)).astype(BF16)
+        taps[:, QW * q : QW * q + QW] = dot(w_v[3].reshape(9 * CB, C), joined[q])
+    wait_bytes(rb.at[3], rim_recv.at[3])
+    wait_bytes(rb.at[3], rim_send.at[3])
+    coarse_wait(g5, coarse_send.at[2])
     rims = rim_sums(3, S1, exp1)
     for rows in range(0, CB, 16):
         act = gelu(conv_rows(3, S1, rows, rims))
         own = pl.ds(pl.multiple_of(chan * CB + rows, 16), 16)
         for q in range(Q):
-            field = g4[q, own, :].astype(F32)
+            field = joined[q, own, :].astype(F32)
             out_ref[rows : rows + 16, QW * q : QW * q + QW] = (
                 field + act[:, QW * q : QW * q + QW]
             ).astype(BF16)
-    for copy in sent:
-        copy.wait_send()
 
 
 def on_device(
@@ -401,14 +424,16 @@
     return pl.pallas_call(
         functools.partial(kernel, tiles),
         out_shape=jax.ShapeDtypeStruct((CB, S1 * S1), BF16),
-        in_specs=[pl.BlockSpec(memory_space=pltpu.MemorySpace.SMEM)] + [hbm] * 9,
+        in_specs=[hbm] * 10,
         out_specs=vmem,
         scratch_shapes=[
+            pltpu.SMEM((4, tiles), jnp.int32),
             pltpu.VMEM((Q, C, QW), BF16),
             pltpu.VMEM((C, QW), BF16),
             pltpu.VMEM((C, QW), BF16),
             pltpu.VMEM((Q, C, QW), BF16),
-            pltpu.VMEM((Q, CB, QW), BF16),
+            pltpu.VMEM((C, QW), BF16),
+            pltpu.VMEM((Q, C, QW), BF16),
             pltpu.VMEM((4, 9, CB, C), BF16),
             pltpu.VMEM((4, 1, CB), F32),
             pltpu.VMEM((4, CB, 128), F32),
@@ -417,18 +442,21 @@
             pltpu.VMEM((128, S1 * S1), BF16),
             pltpu.VMEM((128, S2 * S2), BF16),
             pltpu.VMEM((QW, QW), BF16),
+            pltpu.VMEM((Q, QW, QW), BF16),
             pltpu.VMEM((4, 4, 16, 128), BF16),
             pltpu.VMEM((4, PEERS, 4, 16, 128), BF16),
             pltpu.VMEM((9 * CB, S1 * S1), F32),
-            dma((Q,)),
+            dma,
+            dma,
             dma((4,)),
             dma((4,)),
-            dma((2, 3, Q)),
-            dma((2, 3, Q)),
             dma((2, 3)),
-            dma((2, 3)),
-            dma((4, PEERS, 4)),
-            dma((4, PEERS, 4)),
+            dma((2,)),
+            dma((2, 2, Q)),
+            dma((3,)),
+            dma((3,)),
+            dma((4,)),
+            dma((4,)),
         ],
         compiler_params=pltpu.CompilerParams(
             collective_id=0, has_side_effects=True, vmem_limit_bytes=62 * 1024 * 1024

time: 55.7 us -> 58.1 us (1.043)
  Pallas kernels: 53.9 us -> 56.3 us
    pallas_call x1, Pallas kernels: 53.9 us -> 56.3 us  [on_device(): pl.pallas_call(functools.partial(kernel, tiles), out_shape=jax.ShapeDtype...]
where the time goes in v2:
time: 58.1 us; the launch traced here: 57.9 us
  Pallas kernels  56.3 us (97%)
  local copies, waits for them, and re-layouts  1.57 us (3%)
    pallas_call x1, Pallas kernels, on_device(): pl.pallas_call(functools.partial(kernel, tiles), out_shape=jax.ShapeDtype...  56.3 us
    unnamed x1, local copies, waits for them, and re-layouts  1.57 us

profile of v2, /device:TPU:1, one launch (start us, length us, event | category | flops | bytes accessed | tf_op | source)
XLA Modules:
  0.0 57.9 jit_solution(9601460119862137039)
XLA Ops:
  0.0 56.3 %unet_window.1 = bf16[64,1024]{1,0:T(8,128)(2,1)} custom-call(s32[4,128]{1,0:T(4,128)} %bitcast.5, bf16[64,1024]{1,0:T(8,128)(2,1)} %x_hbm.1, bf16[9,64,256]{2,1,0:T(8,128)(2,1)} %w0_hbm.1, bf16[9,64,256]{2,1,0:T(8,128)(2,1)} %w1_hbm.1, bf16[9,64,256]{2,1,0:T(8,128)(2,1)} %w2_hbm.1, bf16[9,64,256]{2,1,0:T(8,128)(2,1)} %w3_hbm.1, f32[1,64]{1,0:T(1,128)} %bitcast.6, ...), custom_call_target="tpu_custom_call" | custom-call | tf_op jit(solution)/shard_map/unet_window/pallas_call | solution.py:424
  56.4 1.6 %copy.12 = bf16[64,1024]{1,0:T(8,128)(2,1)} copy(bf16[64,1024]{1,0:T(8,128)(2,1)} %unet_window.1) | data formatting | bytes 262144

commit v3 on v2

--- a/solution.py
+++ b/solution.py
@@ -32,10 +32,6 @@
 
 def dot(a, b):
     return lax.dot_general(a, b, (((1,), (0,)), ((), ())), preferred_element_type=F32)
-
-
-def dot_t(a, b):
-    return lax.dot_general(a, b, (((1,), (1,)), ((), ())), preferred_element_type=F32)
 
 
 def one_hot(cond):
@@ -86,6 +82,7 @@
     sb,
     rb,
     taps,
+    pre,
     codes_sem,
     x_sem,
     w_sem,
@@ -275,7 +272,7 @@
         spread = dot(jnp.concatenate([high, low], axis=0), exp[...])
         return spread[:CB] + spread[CB:]
 
-    def conv_rows(layer, size, rows, rims):
+    def conv_rows(layer, size, rows):
         cells = size * size
         place = iota((1, cells), 1)
         column = place % size
@@ -288,12 +285,16 @@
         left = jnp.where(column == 0, 0.0, pltpu.roll(sums[0], 1, 1))
         right = jnp.where(column == size - 1, 0.0, pltpu.roll(sums[2], cells - 1, 1))
         bias = bias_v[layer, rows : rows + 16, 0:1]
-        return (sums[1] + (left + right)) + (rims[rows : rows + 16, :] + bias)
+        pre[rows : rows + 16, :cells] = (sums[1] + (left + right)) + bias
+
+    def inner_sums(layer, size):
+        for rows in range(0, CB, 16):
+            conv_rows(layer, size, rows)
+
+    def activation(size, rows, rims):
+        return gelu(pre[rows : rows + 16, : size * size] + rims[rows : rows + 16, :])
 
     to_partner, to_across, relay = fine_copies(0, g1, lambda q: x_hbm.at[:, pl.ds(q * QW, QW)])
-    pl.semaphore_wait(barrier, 3 + 4 * PEERS)
-    for copy in to_across + to_partner:
-        copy.start()
     for copy in b_copies + w_copies:
         copy.start()
     codes_copy.wait()
@@ -307,7 +308,10 @@
     wait_bytes(g1.at[:, mine, :], x_sem)
     picked = sum(dot(g1[q, mine, :], sel1[QW * q : QW * q + QW, :]) for q in range(Q))
     pack_rims(0, picked)
+    pl.semaphore_wait(barrier, 3 + 4 * PEERS)
     for copy in rim_copies(0):
+        copy.start()
+    for copy in to_across + to_partner:
         copy.start()
     pick_table(code, S2, sel2)
     other_tables()
@@ -319,10 +323,11 @@
     for q in range(Q):
         relay[q].wait_recv()
         taps[:, QW * q : QW * q + QW] = dot(w_v[0].reshape(9 * CB, C), g1[q])
+    inner_sums(0, S1)
     wait_bytes(rb.at[0], rim_recv.at[0])
     rims = rim_sums(0, S1, exp1)
     for rows in range(0, CB, 16):
-        act = gelu(conv_rows(0, S1, rows, rims))
+        act = activation(S1, rows, rims)
         own = pl.ds(pl.multiple_of(chan * CB + rows, 16), 16)
         for q in range(Q):
             field = g1[q, own, :].astype(F32)
@@ -338,35 +343,31 @@
     middle = coarse
     for layer, g in ((1, g2), (2, g3)):
         g[mine, :] = middle
-        for copy in coarse_copies(layer - 1, g):
-            copy.start()
         pack_rims(layer, dot(middle, sel2[...]))
         for copy in rim_copies(layer):
             copy.start()
+        for copy in coarse_copies(layer - 1, g):
+            copy.start()
         if layer == 1:
-            for copy in to_across[: Q // 2] + to_partner:
+            for copy in to_across + to_partner:
                 copy.start()
+        else:
+            for q in range(Q):
+                to_across[q].wait_recv()
+                relay[q].start()
         w_copies[layer].wait()
         coarse_wait(g, coarse_recv.at[layer - 1])
         taps[:, :QW] = dot(w_v[layer].reshape(9 * CB, C), g[...])
+        inner_sums(layer, S2)
         wait_bytes(rb.at[layer], rim_recv.at[layer])
-        if layer == 1:
-            for copy in to_across[Q // 2 :]:
-                copy.start()
-        half = range(Q // 2 * (layer - 1), Q // 2 * layer)
-        for q in half:
-            to_across[q].wait_recv()
-            relay[q].start()
         rims = rim_sums(layer, S2, exp2)
         parts = []
         for rows in range(0, CB, 16):
-            act = gelu(conv_rows(layer, S2, rows, rims))
+            act = activation(S2, rows, rims)
             parts.append((middle[rows : rows + 16, :].astype(F32) + act).astype(BF16))
         middle = jnp.concatenate(parts, axis=0)
 
     g5[mine, :] = middle
-    for copy in coarse_copies(2, g5):
-        copy.start()
     picked = None
     for q in range(Q):
         own = (dot(middle, up[q]) + g4[q, mine, :].astype(F32)).astype(BF16)
@@ -374,6 +375,8 @@
         picked = part if picked is None else picked + part
     pack_rims(3, picked)
     for copy in rim_copies(3):
+        copy.start()
+    for copy in coarse_copies(2, g5):
         copy.start()
     w_copies[3].wait()
     wait_bytes(g4.at[:, mine, :], partner_recv.at[1])
@@ -390,12 +393,13 @@
     for q in range(Q):
         joined[q] = (dot(g5[...], up[q]) + g4[q].astype(F32)).astype(BF16)
         taps[:, QW * q : QW * q + QW] = dot(w_v[3].reshape(9 * CB, C), joined[q])
-    wait_bytes(rb.at[3], rim_recv.at[3])
+    inner_sums(3, S1)
     wait_bytes(rb.at[3], rim_send.at[3])
     coarse_wait(g5, coarse_send.at[2])
+    wait_bytes(rb.at[3], rim_recv.at[3])
     rims = rim_sums(3, S1, exp1)
     for rows in range(0, CB, 16):
-        act = gelu(conv_rows(3, S1, rows, rims))
+        act = activation(S1, rows, rims)
         own = pl.ds(pl.multiple_of(chan * CB + rows, 16), 16)
         for q in range(Q):
             field = joined[q, own, :].astype(F32)
@@ -423,7 +427,7 @@
     biases = [b.reshape(1, CB) for b in (bias_enc, bias_mid_a, bias_mid_b, bias_dec)]
     return pl.pallas_call(
         functools.partial(kernel, tiles),
-        out_shape=jax.ShapeDtypeStruct((CB, S1 * S1), BF16),
+        out_shape=pltpu.MemorySpace.VMEM((CB, S1 * S1), BF16),
         in_specs=[hbm] * 10,
         out_specs=vmem,
         scratch_shapes=[
@@ -446,6 +450,7 @@
             pltpu.VMEM((4, 4, 16, 128), BF16),
             pltpu.VMEM((4, PEERS, 4, 16, 128), BF16),
             pltpu.VMEM((9 * CB, S1 * S1), F32),
+            pltpu.VMEM((CB, S1 * S1), F32),
             dma,
             dma,
             dma((4,)),

time: 58.1 us -> 49 us (0.84)
  Pallas kernels: 56.3 us -> 48.2 us
  local copies, waits for them, and re-layouts: 1.57 us -> 0.66 us
    pallas_call x1, Pallas kernels: 56.3 us -> 48.2 us  [on_device(): pl.pallas_call(functools.partial(kernel, tiles), out_shape=pltpu.MemorySp...]
    unnamed x1, local copies, waits for them, and re-layouts: 1.57 us -> 0.66 us
where the time goes in v3:
time: 49 us; the launch traced here: 48.9 us
  Pallas kernels  48.2 us (98%)
  local copies, waits for them, and re-layouts  0.66 us (1%)
    pallas_call x1, Pallas kernels, on_device(): pl.pallas_call(functools.partial(kernel, tiles), out_shape=pltpu.MemorySp...  48.2 us

profile of v3, /device:TPU:1, one launch (start us, length us, event | category | flops | bytes accessed | tf_op | source)
XLA Modules:
  0.0 48.9 jit_solution(18295351655959067581)
XLA Ops:
  0.0 48.2 %unet_window.1 = bf16[64,1024]{1,0:T(8,128)(2,1)S(1)} custom-call(s32[4,128]{1,0:T(4,128)} %bitcast.5, bf16[64,1024]{1,0:T(8,128)(2,1)} %x_hbm.1, bf16[9,64,256]{2,1,0:T(8,128)(2,1)} %w0_hbm.1, bf16[9,64,256]{2,1,0:T(8,128)(2,1)} %w1_hbm.1, bf16[9,64,256]{2,1,0:T(8,128)(2,1)} %w2_hbm.1, bf16[9,64,256]{2,1,0:T(8,128)(2,1)} %w3_hbm.1, f32[1,64]{1,0:T(1,128)} %bitcast.6, ...), custom_call_target="tpu_custom_call" | custom-call | tf_op jit(solution)/shard_map/unet_window/pallas_call | solution.py:428
  48.2 0.7 %copy.12 = bf16[64,1024]{1,0:T(8,128)(2,1)} copy(bf16[64,1024]{1,0:T(8,128)(2,1)S(1)} %unet_window.1) | data formatting | bytes 262144

commit v4 on v3

--- a/solution.py
+++ b/solution.py
@@ -74,7 +74,12 @@
     b_v,
     bias_v,
     sel1,
-    sel2,
+    sel_enc,
+    sel_a,
+    sel_b,
+    nxt_enc,
+    nxt_a,
+    nxt_b,
     exp1,
     exp2,
     pool,
@@ -141,10 +146,17 @@
     def wait_bytes(ref, sem):
         pltpu.make_async_copy(ref, ref, sem).wait()
 
-    def pick_table(code, size, sel):
-        place = jnp.where(code >= 4, size - 1 - along, along)
-        cell = jnp.where(along < size, edge_position(code % 4, place, size), -1)
-        sel[...] = one_hot(iota((size * size, 128), 0) == cell)
+    def pick_tables(code):
+        edge = code % 4
+        place = jnp.where(code >= 4, S2 - 1 - along, along)
+        cell = edge_position(edge, place, S2)
+        sel_a[...] = one_hot(iota((S2 * S2, 128), 0) == jnp.where(along < S2, cell, -1))
+        corner = 2 * (cell // S2) * S1 + 2 * (cell % S2)
+        for part in range(4):
+            fine = jnp.where(along < S2, corner + part // 2 * S1 + part % 2, -1)
+            sel_enc[:, 128 * part : 128 * part + 128] = one_hot(iota((S1 * S1, 128), 0) == fine)
+        place = jnp.where(code >= 4, S1 - 1 - along, along)
+        sel_b[...] = one_hot(iota((S2 * S2, 128), 0) == edge_position(edge, place // 2, S2))
 
     def other_tables():
         row = iota((128, 1), 0)
@@ -153,6 +165,9 @@
                 row % 32 < size, edge_position(row // 32, row % 32, size), -1
             )
             exp[...] = one_hot(iota((128, size * size), 1) == cell)
+        nxt_enc[...] = dot(exp1[...], sel_enc[...]).astype(BF16)
+        nxt_a[...] = dot(exp2[...], sel_a[...]).astype(BF16)
+        nxt_b[...] = dot(exp2[...], sel_b[...]).astype(BF16)
         cell = iota((QW, QW), 0)
         pool[...] = one_hot(
             (cell // S1 // 2) * S2 + (cell % S1) // 2 == iota((QW, QW), 1) % (QW // 4)
@@ -183,9 +198,8 @@
 
     def rim_copies(layer):
         copies = []
-        for step in range(PEERS):
+        for peer in (across, diagonal, partner, chan):
             for side in range(4):
-                peer = (chan + step) % PEERS
                 copies.append(
                     pltpu.make_async_remote_copy(
                         src_ref=sb.at[layer, side],
@@ -240,7 +254,15 @@
     def coarse_wait(g, sem):
         wait_bytes(g.at[pl.ds(0, 3 * CB), :], sem)
 
-    def rim_sums(layer, size, exp):
+    def in_two(v):
+        high = v.astype(BF16)
+        return jnp.concatenate([high, (v - high.astype(F32)).astype(BF16)], axis=0)
+
+    def take(two, table):
+        both = dot(two, table)
+        return both[:CB] + both[CB:]
+
+    def rim_sums(layer, size):
         blocks = []
         for source in range(PEERS):
             parts = [rb[layer, source, side].astype(F32) for side in range(4)]
@@ -267,10 +289,7 @@
         before = jnp.where(along == 0, 0.0, pltpu.roll(by_side(0, 6, 0, 2), 1, 1))
         after = jnp.where(along == size - 1, 0.0, pltpu.roll(by_side(2, 8, 6, 8), 127, 1))
         total = before + by_side(1, 7, 3, 5) + after
-        high = total.astype(BF16)
-        low = (total - high.astype(F32)).astype(BF16)
-        spread = dot(jnp.concatenate([high, low], axis=0), exp[...])
-        return spread[:CB] + spread[CB:]
+        return in_two(total)
 
     def conv_rows(layer, size, rows):
         cells = size * size
@@ -304,7 +323,9 @@
         codes_here[0],
         jnp.where(slot == 1, codes_here[1], jnp.where(slot == 2, codes_here[2], codes_here[3])),
     )
-    pick_table(code, S1, sel1)
+    place = jnp.where(code >= 4, S1 - 1 - along, along)
+    cell = edge_position(code % 4, place, S1)
+    sel1[...] = one_hot(iota((S1 * S1, 128), 0) == cell)
     wait_bytes(g1.at[:, mine, :], x_sem)
     picked = sum(dot(g1[q, mine, :], sel1[QW * q : QW * q + QW, :]) for q in range(Q))
     pack_rims(0, picked)
@@ -313,7 +334,7 @@
         copy.start()
     for copy in to_across + to_partner:
         copy.start()
-    pick_table(code, S2, sel2)
+    pick_tables(code)
     other_tables()
     w_copies[0].wait()
     for q in range(Q):
@@ -324,8 +345,16 @@
         relay[q].wait_recv()
         taps[:, QW * q : QW * q + QW] = dot(w_v[0].reshape(9 * CB, C), g1[q])
     inner_sums(0, S1)
+    sums = take(in_two(pre[...]), sel_enc[...])
+    field = sum(dot(g1[q, mine, :], sel_enc[QW * q : QW * q + QW, :]) for q in range(Q))
     wait_bytes(rb.at[0], rim_recv.at[0])
-    rims = rim_sums(0, S1, exp1)
+    two = rim_sums(0, S1)
+    edge = (field + gelu(sums + take(two, nxt_enc[...]))).astype(BF16).astype(F32)
+    edge = (edge[:, :128] + edge[:, 128:256]) + (edge[:, 256:384] + edge[:, 384:])
+    pack_rims(1, edge * 0.25)
+    for copy in rim_copies(1):
+        copy.start()
+    rims = take(two, exp1[...])
     for rows in range(0, CB, 16):
         act = activation(S1, rows, rims)
         own = pl.ds(pl.multiple_of(chan * CB + rows, 16), 16)
@@ -341,11 +370,9 @@
         coarse = jnp.where(group == q, pooled[CB * q : CB * q + CB], coarse)
     coarse = (coarse * 0.25).astype(BF16)
     middle = coarse
+    encoded = sum(dot(g4[q, mine, :], sel1[QW * q : QW * q + QW, :]) for q in range(Q))
     for layer, g in ((1, g2), (2, g3)):
         g[mine, :] = middle
-        pack_rims(layer, dot(middle, sel2[...]))
-        for copy in rim_copies(layer):
-            copy.start()
         for copy in coarse_copies(layer - 1, g):
             copy.start()
         if layer == 1:
@@ -359,8 +386,18 @@
         coarse_wait(g, coarse_recv.at[layer - 1])
         taps[:, :QW] = dot(w_v[layer].reshape(9 * CB, C), g[...])
         inner_sums(layer, S2)
+        sel, nxt = ((sel_a, nxt_a), (sel_b, nxt_b))[layer - 1]
+        sums = take(in_two(pre[:, :QW]), sel[...])
+        field = dot(middle, sel[...])
         wait_bytes(rb.at[layer], rim_recv.at[layer])
-        rims = rim_sums(layer, S2, exp2)
+        two = rim_sums(layer, S2)
+        edge = (field + gelu(sums + take(two, nxt[...]))).astype(BF16).astype(F32)
+        if layer == 2:
+            edge = edge + encoded
+        pack_rims(layer + 1, edge)
+        for copy in rim_copies(layer + 1):
+            copy.start()
+        rims = take(two, exp2[...])
         parts = []
         for rows in range(0, CB, 16):
             act = activation(S2, rows, rims)
@@ -368,14 +405,6 @@
         middle = jnp.concatenate(parts, axis=0)
 
     g5[mine, :] = middle
-    picked = None
-    for q in range(Q):
-        own = (dot(middle, up[q]) + g4[q, mine, :].astype(F32)).astype(BF16)
-        part = dot(own, sel1[QW * q : QW * q + QW, :])
-        picked = part if picked is None else picked + part
-    pack_rims(3, picked)
-    for copy in rim_copies(3):
-        copy.start()
     for copy in coarse_copies(2, g5):
         copy.start()
     w_copies[3].wait()
@@ -397,7 +426,7 @@
     wait_bytes(rb.at[3], rim_send.at[3])
     coarse_wait(g5, coarse_send.at[2])
     wait_bytes(rb.at[3], rim_recv.at[3])
-    rims = rim_sums(3, S1, exp1)
+    rims = take(rim_sums(3, S1), exp1[...])
     for rows in range(0, CB, 16):
         act = activation(S1, rows, rims)
         own = pl.ds(pl.multiple_of(chan * CB + rows, 16), 16)
@@ -442,7 +471,12 @@
             pltpu.VMEM((4, 1, CB), F32),
             pltpu.VMEM((4, CB, 128), F32),
             pltpu.VMEM((S1 * S1, 128), BF16),
+            pltpu.VMEM((S1 * S1, 4 * 128), BF16),
             pltpu.VMEM((S2 * S2, 128), BF16),
+            pltpu.VMEM((S2 * S2, 128), BF16),
+            pltpu.VMEM((128, 4 * 128), BF16),
+            pltpu.VMEM((128, 128), BF16),
+            pltpu.VMEM((128, 128), BF16),
             pltpu.VMEM((128, S1 * S1), BF16),
             pltpu.VMEM((128, S2 * S2), BF16),
             pltpu.VMEM((QW, QW), BF16),

time: 49 us -> 48.1 us (0.982)
  Pallas kernels: 48.2 us -> 47.3 us
    pallas_call x1, Pallas kernels: 48.2 us -> 47.3 us  [on_device(): pl.pallas_call(functools.partial(kernel, tiles), out_shape=pltpu.MemorySp...]
where the time goes in v4:
time: 48.1 us; the launch traced here: 48 us
  Pallas kernels  47.3 us (98%)
  local copies, waits for them, and re-layouts  0.66 us (1%)
    pallas_call x1, Pallas kernels, on_device(): pl.pallas_call(functools.partial(kernel, tiles), out_shape=pltpu.MemorySp...  47.3 us

profile of v4, /device:TPU:1, one launch (start us, length us, event | category | flops | bytes accessed | tf_op | source)
XLA Modules:
  0.0 48.0 jit_solution(12149927234733219832)
XLA Ops:
  0.0 47.3 %unet_window.1 = bf16[64,1024]{1,0:T(8,128)(2,1)S(1)} custom-call(s32[4,128]{1,0:T(4,128)} %bitcast.5, bf16[64,1024]{1,0:T(8,128)(2,1)} %x_hbm.1, bf16[9,64,256]{2,1,0:T(8,128)(2,1)} %w0_hbm.1, bf16[9,64,256]{2,1,0:T(8,128)(2,1)} %w1_hbm.1, bf16[9,64,256]{2,1,0:T(8,128)(2,1)} %w2_hbm.1, bf16[9,64,256]{2,1,0:T(8,128)(2,1)} %w3_hbm.1, f32[1,64]{1,0:T(1,128)} %bitcast.6, ...), custom_call_target="tpu_custom_call" | custom-call | tf_op jit(solution)/shard_map/unet_window/pallas_call | solution.py:457
  47.3 0.7 %copy.12 = bf16[64,1024]{1,0:T(8,128)(2,1)} copy(bf16[64,1024]{1,0:T(8,128)(2,1)S(1)} %unet_window.1) | data formatting | bytes 262144

commit v5 on v4

--- a/solution.py
+++ b/solution.py
@@ -96,6 +96,7 @@
     partner_recv,
     fine_recv,
     coarse_send,
+    across_recv,
     coarse_recv,
     rim_send,
     rim_recv,
@@ -239,17 +240,30 @@
         )
 
     def coarse_copies(index, g):
-        return [
-            pltpu.make_async_remote_copy(
-                src_ref=g.at[mine, :],
-                dst_ref=g.at[mine, :],
+        def copy_to(peer, rows, recv):
+            return pltpu.make_async_remote_copy(
+                src_ref=g.at[rows, :],
+                dst_ref=g.at[rows, :],
                 send_sem=coarse_send.at[index],
-                recv_sem=coarse_recv.at[index],
+                recv_sem=recv,
                 device_id=(tile, peer),
                 device_id_type=MESH,
             )
-            for peer in (across, diagonal, partner)
-        ]
+
+        return (
+            copy_to(across, mine, across_recv.at[index]),
+            copy_to(partner, mine, coarse_recv.at[index]),
+            copy_to(partner, across_rows, coarse_recv.at[index]),
+        )
+
+    def coarse_start(copies):
+        copies[0].start()
+        copies[1].start()
+
+    def coarse_relay(copies, index, g):
+        copies[0].wait_recv()
+        copies[2].start()
+        wait_bytes(g.at[pl.ds(0, 2 * CB), :], coarse_recv.at[index])
 
     def coarse_wait(g, sem):
         wait_bytes(g.at[pl.ds(0, 3 * CB), :], sem)
@@ -373,8 +387,8 @@
     encoded = sum(dot(g4[q, mine, :], sel1[QW * q : QW * q + QW, :]) for q in range(Q))
     for layer, g in ((1, g2), (2, g3)):
         g[mine, :] = middle
-        for copy in coarse_copies(layer - 1, g):
-            copy.start()
+        coarse = coarse_copies(layer - 1, g)
+        coarse_start(coarse)
         if layer == 1:
             for copy in to_across + to_partner:
                 copy.start()
@@ -383,7 +397,7 @@
                 to_across[q].wait_recv()
                 relay[q].start()
         w_copies[layer].wait()
-        coarse_wait(g, coarse_recv.at[layer - 1])
+        coarse_relay(coarse, layer - 1, g)
         taps[:, :QW] = dot(w_v[layer].reshape(9 * CB, C), g[...])
         inner_sums(layer, S2)
         sel, nxt = ((sel_a, nxt_a), (sel_b, nxt_b))[layer - 1]
@@ -405,8 +419,8 @@
         middle = jnp.concatenate(parts, axis=0)
 
     g5[mine, :] = middle
-    for copy in coarse_copies(2, g5):
-        copy.start()
+    coarse = coarse_copies(2, g5)
+    coarse_start(coarse)
     w_copies[3].wait()
     wait_bytes(g4.at[:, mine, :], partner_recv.at[1])
     for q in range(Q):
@@ -418,7 +432,7 @@
         wait_bytes(rb.at[layer], rim_send.at[layer])
     for index in range(2):
         coarse_wait(g2, coarse_send.at[index])
-    coarse_wait(g5, coarse_recv.at[2])
+    coarse_relay(coarse, 2, g5)
     for q in range(Q):
         joined[q] = (dot(g5[...], up[q]) + g4[q].astype(F32)).astype(BF16)
         taps[:, QW * q : QW * q + QW] = dot(w_v[3].reshape(9 * CB, C), joined[q])
@@ -494,6 +508,7 @@
             dma((2, 2, Q)),
             dma((3,)),
             dma((3,)),
+            dma((3,)),
             dma((4,)),
             dma((4,)),
         ],

time: 48.1 us -> 48.1 us (level)
  no operation moved by 1% of the time
where the time goes in v5:
time: 48.1 us; the launch traced here: 48 us
  Pallas kernels  47.3 us (98%)
  local copies, waits for them, and re-layouts  0.66 us (1%)
    pallas_call x1, Pallas kernels, on_device(): pl.pallas_call(functools.partial(kernel, tiles), out_shape=pltpu.MemorySp...  47.3 us

profile of v5, /device:TPU:1, one launch (start us, length us, event | category | flops | bytes accessed | tf_op | source)
XLA Modules:
  0.0 48.0 jit_solution(10229472602246504906)
XLA Ops:
  0.0 47.3 %unet_window.1 = bf16[64,1024]{1,0:T(8,128)(2,1)S(1)} custom-call(s32[4,128]{1,0:T(4,128)} %bitcast.5, bf16[64,1024]{1,0:T(8,128)(2,1)} %x_hbm.1, bf16[9,64,256]{2,1,0:T(8,128)(2,1)} %w0_hbm.1, bf16[9,64,256]{2,1,0:T(8,128)(2,1)} %w1_hbm.1, bf16[9,64,256]{2,1,0:T(8,128)(2,1)} %w2_hbm.1, bf16[9,64,256]{2,1,0:T(8,128)(2,1)} %w3_hbm.1, f32[1,64]{1,0:T(1,128)} %bitcast.6, ...), custom_call_target="tpu_custom_call" | custom-call | tf_op jit(solution)/shard_map/unet_window/pallas_call | solution.py:471
  47.3 0.7 %copy.12 = bf16[64,1024]{1,0:T(8,128)(2,1)} copy(bf16[64,1024]{1,0:T(8,128)(2,1)S(1)} %unet_window.1) | data formatting | bytes 262144

commit v6 on v4

--- a/solution.py
+++ b/solution.py
@@ -115,14 +115,14 @@
     across_rows = pl.ds(pl.multiple_of(across * CB, CB), CB)
 
     barrier = pltpu.get_barrier_semaphore()
-    for peer in (partner, across, diagonal):
-        pl.semaphore_signal(barrier, inc=1, device_id=(tile, peer), device_id_type=MESH)
-    for side in range(4):
-        for step in range(PEERS):
-            peer = (chan + step) % PEERS
+    for peer in (across, diagonal, partner, chan):
+        for side in (3, 2, 1, 0):
             pl.semaphore_signal(
                 barrier, inc=1, device_id=(near[side], peer), device_id_type=MESH
             )
+
+    for peer in (partner, across, diagonal):
+        pl.semaphore_signal(barrier, inc=1, device_id=(tile, peer), device_id_type=MESH)
 
     codes_copy = pltpu.make_async_copy(codes_hbm, codes, codes_sem)
     codes_copy.start()
@@ -199,7 +199,7 @@
     def rim_copies(layer):
         copies = []
         for peer in (across, diagonal, partner, chan):
-            for side in range(4):
+            for side in (3, 2, 1, 0):
                 copies.append(
                     pltpu.make_async_remote_copy(
                         src_ref=sb.at[layer, side],

time: 48.1 us -> 47.7 us (level)
  no operation moved by 1% of the time
where the time goes in v6:
time: 47.7 us; the launch traced here: 47.6 us
  Pallas kernels  46.9 us (98%)
  local copies, waits for them, and re-layouts  0.66 us (1%)
    pallas_call x1, Pallas kernels, on_device(): pl.pallas_call(functools.partial(kernel, tiles), out_shape=pltpu.MemorySp...  46.9 us

profile of v6, /device:TPU:1, one launch (start us, length us, event | category | flops | bytes accessed | tf_op | source)
XLA Modules:
  0.0 47.6 jit_solution(4257545502924780081)
XLA Ops:
  0.0 46.9 %unet_window.1 = bf16[64,1024]{1,0:T(8,128)(2,1)S(1)} custom-call(s32[4,128]{1,0:T(4,128)} %bitcast.5, bf16[64,1024]{1,0:T(8,128)(2,1)} %x_hbm.1, bf16[9,64,256]{2,1,0:T(8,128)(2,1)} %w0_hbm.1, bf16[9,64,256]{2,1,0:T(8,128)(2,1)} %w1_hbm.1, bf16[9,64,256]{2,1,0:T(8,128)(2,1)} %w2_hbm.1, bf16[9,64,256]{2,1,0:T(8,128)(2,1)} %w3_hbm.1, f32[1,64]{1,0:T(1,128)} %bitcast.6, ...), custom_call_target="tpu_custom_call" | custom-call | tf_op jit(solution)/shard_map/unet_window/pallas_call | solution.py:457
  46.9 0.7 %copy.12 = bf16[64,1024]{1,0:T(8,128)(2,1)} copy(bf16[64,1024]{1,0:T(8,128)(2,1)S(1)} %unet_window.1) | data formatting | bytes 262144
